TPU v7x, 512 devices: a whole 4x4x16 slice. The times are simulated.
512 devices in a mesh: tm: 16 (over x, z_hi, core), gy: 8 (over z_lo), gx: 4 (over y).
Axes of the slice: x: 4, y: 4, z: 16 (z_hi: 2, z_lo: 8; z = z_hi * 8 + z_lo), core: 2. Of those that a mesh axis runs over, the one named last changes fastest.
Arguments:
- initial_state: float32 [2, 32, 64, 128], P(None, 'gy', 'gx'), may hold values from 0 to 1
- slice_guess: float32 [16, 2, 32, 64, 128], P('tm', None, 'gy', 'gx'), may hold values from 0 to 1
- feed_rate: float32 [32, 64, 128], P('gy', 'gx'), may hold values from 0.02 to 0.2
- kill_rate: float32 [32, 64, 128], P('gy', 'gx'), may hold values from 0.03 to 0.12
Outputs:
- final_states: float32 [16, 2, 32, 64, 128], P('tm', None, 'gy', 'gx')
All inputs are finite; a program needn't handle non-finite values.
Results may differ from a plain program's by a relative error of at most 0.0001.
Values sent between devices are 32-bit elements; how exact they have to be, the bound alone decides.
A program may use at most 64 MiB of HBM per device.

v0:
```python
import jax
import jax.numpy as jnp
from jax import lax
from jax.sharding import PartitionSpec as P

ITERS = 3


DIFF_U = 0.2
DIFF_V = 0.1
HALF_STEP = 0.5
WEIGHTS = ((5.0 / 24.0, 8.0 / 24.0, -1.0 / 24.0), (-1.0 / 24.0, 8.0 / 24.0, 5.0 / 24.0))


def from_behind(value, axis, steps):
    count = lax.axis_size(axis)
    first, last = (max(0, -steps), min(count, count - steps))
    return lax.ppermute(value, axis, [(source, source + steps) for source in range(first, last)])


def with_halo(shard, sides, width):
    for axis, dim in sides:
        count, length = (lax.axis_size(axis), shard.shape[dim])
        up = [(i, (i + 1) % count) for i in range(count)]
        down = [(j, i) for i, j in up]
        last = lax.slice_in_dim(shard, length - width, length, axis=dim)
        first = lax.slice_in_dim(shard, 0, width, axis=dim)
        before = lax.ppermute(last, axis, up)
        after = lax.ppermute(first, axis, down)
        shard = jnp.concatenate([before, shard, after], axis=dim)
    return shard


def restrict(grid_field):
    leading = grid_field.shape[:-3]
    size_x, size_y, size_z = grid_field.shape[-3:]
    blocks = grid_field.reshape(leading + (size_x // 2, 2, size_y // 2, 2, size_z // 2, 2))
    return 0.125 * jnp.sum(blocks, axis=(-5, -3, -1))


def prolong(grid_field):
    return jnp.repeat(jnp.repeat(jnp.repeat(grid_field, 2, axis=-3), 2, axis=-2), 2, axis=-1)


def source_terms(laplacian, state, feed_rate, kill_rate):
    conc_u = state[..., 0, :, :, :]
    conc_v = state[..., 1, :, :, :]
    reaction = conc_u * conc_v * conc_v
    rate_u = DIFF_U * laplacian[..., 0, :, :, :] - reaction + feed_rate * (1.0 - conc_u)
    rate_v = DIFF_V * laplacian[..., 1, :, :, :] + reaction - (feed_rate + kill_rate) * conc_v
    return jnp.stack([rate_u, rate_v], axis=-4)


def halo_rates(padded, feed_rate, kill_rate, spacing):
    center = padded[..., 1:-1, 1:-1, :]
    summed = -6.0 * center
    summed = summed + padded[..., :-2, 1:-1, :] + padded[..., 2:, 1:-1, :]
    summed = summed + padded[..., 1:-1, :-2, :] + padded[..., 1:-1, 2:, :]
    summed = summed + jnp.roll(center, 1, -1) + jnp.roll(center, -1, -1)
    return source_terms(summed / (spacing * spacing), center, feed_rate, kill_rate)


def quadrature(values, interval):
    return (
        WEIGHTS[interval][0] * values[0]
        + WEIGHTS[interval][1] * values[1]
        + WEIGHTS[interval][2] * values[2]
    )


def shards(initial_state, slice_guess, feed_rate, kill_rate):
    is_first = lax.axis_index("tm") == 0
    coarse_feed = restrict(feed_rate)
    coarse_kill = restrict(kill_rate)
    guess_state = slice_guess[0]
    guess_rates = jnp.zeros_like(guess_state)
    node_values = [guess_state, guess_state, guess_state]
    values = [guess_rates, guess_rates, guess_rates]
    coarse_end = restrict(guess_state)
    coarse_anchor = restrict(initial_state)
    for sweep_index in range(ITERS):
        integral_one = quadrature(values, 1)
        got_state, got_coarse = from_behind((node_values[2], coarse_end), "tm", 1)
        start_state = jnp.where(is_first, initial_state, got_state)
        coarse_start = jnp.where(is_first, coarse_anchor, got_coarse)
        rate_zero = halo_rates(
            with_halo(start_state, (("gy", 1), ("gx", 2)), 1), feed_rate, kill_rate, 1.0
        )
        node_one = start_state + HALF_STEP * (rate_zero - values[0]) + quadrature(values, 0)
        rate_one = halo_rates(
            with_halo(node_one, (("gy", 1), ("gx", 2)), 1), feed_rate, kill_rate, 1.0
        )
        node_two = node_one + HALF_STEP * (rate_one - values[1]) + integral_one
        rate_two = halo_rates(
            with_halo(node_two, (("gy", 1), ("gx", 2)), 1), feed_rate, kill_rate, 1.0
        )
        fresh = [rate_zero, rate_one, rate_two]
        fine_zero = quadrature(fresh, 0)
        fine_one = quadrature(fresh, 1)
        rest_zero = restrict(start_state)
        rest_one = restrict(node_one)
        rest_two = restrict(node_two)
        rest_pair = jnp.stack([rest_zero, rest_one])
        coarse_pair = halo_rates(
            with_halo(rest_pair, (("gy", 2), ("gx", 3)), 1), coarse_feed, coarse_kill, 2.0
        )
        start_rates = halo_rates(
            with_halo(coarse_start, (("gy", 1), ("gx", 2)), 1), coarse_feed, coarse_kill, 2.0
        )
        coarse_one = coarse_start + HALF_STEP * (start_rates - coarse_pair[0]) + restrict(fine_zero)
        middle_rates = halo_rates(
            with_halo(coarse_one, (("gy", 1), ("gx", 2)), 1), coarse_feed, coarse_kill, 2.0
        )
        coarse_two = coarse_one + HALF_STEP * (middle_rates - coarse_pair[1]) + restrict(fine_one)
        node_one = node_one + prolong(coarse_one - rest_one)
        node_two = node_two + prolong(coarse_two - rest_two)
        if sweep_index + 1 < ITERS:
            node_pair = jnp.stack([node_one, node_two])
            pair_rates = halo_rates(
                with_halo(node_pair, (("gy", 2), ("gx", 3)), 1), feed_rate, kill_rate, 1.0
            )
            values = [rate_zero, pair_rates[0], pair_rates[1]]
        node_values = [start_state, node_one, node_two]
        coarse_end = coarse_two
    return node_values[2][None]


def solution(mesh):
    in_specs = (
        P(None, "gy", "gx", None),
        P("tm", None, "gy", "gx", None),
        P("gy", "gx", None),
        P("gy", "gx", None),
    )
    out_specs = P("tm", None, "gy", "gx", None)
    return jax.shard_map(shards, mesh=mesh, in_specs=in_specs, out_specs=out_specs, check_vma=False)
```

profile of v0, /device:TPU:30, one launch (start us, length us, event | category | flops | bytes accessed | tf_op | source)
XLA Modules:
  0.0 789.4 jit_solution(16963055211632292899)
XLA Ops:
  3.0 6.3 reshape_squeeze.3
  11.8 15.8 %collective-permute-start.9 = (f32[2,2,8,64]{3,2,1,0:T(8,128)S(1)}, f32[2,2,8,64]{3,2,1,0:T(8,128)S(1)}, u32[]{:S(2)}, u32[]{:S(2)}) collective-permute-start(f32[2,2,8,64]{3,2,1,0:T(8,128)S(1)} %broadcast_multiply_fusion), channel_id=1, source_target_pairs={{0,32},{32,64},{64,96},{96,128},{128,160},{160,192},{192,224},{224... | collective-permute-start | bytes 24584 | tf_op jit(solution)/shard_map/ppermute | solution.py:18
  34.1 5.5 reshape.302
  45.2 9.5 %collective-permute-start.11 = (f32[2,1,8,64]{3,2,1,0:T(8,128)S(1)}, f32[2,1,8,64]{3,2,1,0:T(8,128)S(1)}, u32[]{:S(2)}, u32[]{:S(2)}) collective-permute-start(f32[2,1,8,64]{3,2,1,0:T(8,128)S(1)} %get-tuple-element.242), channel_id=1, source_target_pairs={{4,0},{8,4},{12,8},{16,12},{20,16},{24,20},{28,24},{0,28},{5,1},{9... | collective-permute-start | bytes 12296 | tf_op jit(solution)/shard_map/ppermute | solution.py:29
  69.8 10.8 %collective-permute-start.2 = (f32[2,1,16,128]{2,3,1,0:T(8,128)S(1)}, f32[2,1,16,128]{2,3,1,0:T(8,128)S(1)}, u32[]{:S(2)}, u32[]{:S(2)}) collective-permute-start(f32[2,1,16,128]{2,3,1,0:T(8,128)S(1)} %get-tuple-element.111), channel_id=1, source_target_pairs={{4,0},{8,4},{12,8},{16,12},{20,16},{24,20},{28,24},{0,28},{5,1},{9... | collective-permute-start | bytes 49160 | tf_op jit(solution)/shard_map/ppermute | solution.py:29
  80.8 5.5 reshape.305
  94.3 4.7 collective-permute-start.3
  106.0 5.5 reshape.306
  116.0 10.5 %collective-permute-start.15 = (f32[2,2,1,8,64]{4,3,2,1,0:T(8,128)S(1)}, f32[2,2,1,8,64]{4,3,2,1,0:T(8,128)S(1)}, u32[]{:S(2)}, u32[]{:S(2)}) collective-permute-start(f32[2,2,1,8,64]{4,3,2,1,0:T(8,128)S(1)} %get-tuple-element.206), channel_id=1, source_target_pairs={{4,0},{8,4},{12,8},{16,12},{20,16},{24,20},{28,24},{0,28},{5,1},{9... | collective-permute-start | bytes 24584 | tf_op jit(solution)/shard_map/ppermute | solution.py:29
  128.0 4.4 collective-permute-start.16
  140.9 10.9 %collective-permute-start.6 = (f32[2,1,16,128]{2,3,1,0:T(8,128)S(1)}, f32[2,1,16,128]{2,3,1,0:T(8,128)S(1)}, u32[]{:S(2)}, u32[]{:S(2)}) collective-permute-start(f32[2,1,16,128]{2,3,1,0:T(8,128)S(1)} %get-tuple-element.105), channel_id=1, source_target_pairs={{4,0},{8,4},{12,8},{16,12},{20,16},{24,20},{28,24},{0,28},{5,1},{9... | collective-permute-start | bytes 49160 | tf_op jit(solution)/shard_map/ppermute | solution.py:29
  165.2 5.1 collective-permute-start.7
  185.6 10.7 %collective-permute-start.19 = (f32[2,1,16,128]{2,3,1,0:T(8,128)}, f32[2,1,16,128]{2,3,1,0:T(8,128)S(1)}, u32[]{:S(2)}, u32[]{:S(2)}) collective-permute-start(f32[2,1,16,128]{2,3,1,0:T(8,128)} %get-tuple-element.99), channel_id=1, source_target_pairs={{4,0},{8,4},{12,8},{16,12},{20,16},{24,20},{28,24},{0,28},{5,1},{9... | collective-permute-start | bytes 49160 | tf_op jit(solution)/shard_map/ppermute | solution.py:29
  207.0 5.5 reshape.307
  222.3 5.1 collective-permute-start.20
  247.4 10.5 %collective-permute-start.23 = (f32[2,1,8,64]{3,2,1,0:T(8,128)S(1)}, f32[2,1,8,64]{3,2,1,0:T(8,128)S(1)}, u32[]{:S(2)}, u32[]{:S(2)}) collective-permute-start(f32[2,1,8,64]{3,2,1,0:T(8,128)S(1)} %get-tuple-element.236), channel_id=1, source_target_pairs={{4,0},{8,4},{12,8},{16,12},{20,16},{24,20},{28,24},{0,28},{5,1},{9... | collective-permute-start | bytes 12296 | tf_op jit(solution)/shard_map/ppermute | solution.py:29
  272.0 6.0 collective-permute-start.26
  279.9 10.9 %collective-permute-start.32 = (f32[2,2,1,16,128]{4,3,2,1,0:T(8,128)S(1)}, f32[2,2,1,16,128]{4,3,2,1,0:T(8,128)S(1)}, u32[]{:S(2)}, u32[]{:S(2)}) collective-permute-start(f32[2,2,1,16,128]{4,3,2,1,0:T(8,128)S(1)} %get-tuple-element.135), channel_id=1, source_target_pairs={{4,0},{8,4},{12,8},{16,12},{20,16},{24,20},{28,24},{0,28},{5,1},{9... | collective-permute-start | bytes 98312 | tf_op jit(solution)/shard_map/ppermute | solution.py:29
  292.7 10.5 %collective-permute-start.41 = (f32[2,1,8,64]{3,2,1,0:T(8,128)S(1)}, f32[2,1,8,64]{3,2,1,0:T(8,128)S(1)}, u32[]{:S(2)}, u32[]{:S(2)}) collective-permute-start(f32[2,1,8,64]{3,2,1,0:T(8,128)S(1)} %get-tuple-element.230), channel_id=1, source_target_pairs={{4,0},{8,4},{12,8},{16,12},{20,16},{24,20},{28,24},{0,28},{5,1},{9... | collective-permute-start | bytes 12296 | tf_op jit(solution)/shard_map/ppermute | solution.py:29
  329.1 11.2 %collective-permute-start.28 = (f32[2,1,16,128]{2,3,1,0:T(8,128)S(1)}, f32[2,1,16,128]{2,3,1,0:T(8,128)S(1)}, u32[]{:S(2)}, u32[]{:S(2)}) collective-permute-start(f32[2,1,16,128]{2,3,1,0:T(8,128)S(1)} %get-tuple-element.93), channel_id=1, source_target_pairs={{4,0},{8,4},{12,8},{16,12},{20,16},{24,20},{28,24},{0,28},{5,1},{9... | collective-permute-start | bytes 49160 | tf_op jit(solution)/shard_map/ppermute | solution.py:29
  340.3 5.5 reshape.314
  355.0 5.4 collective-permute-start.29
  370.1 5.5 reshape.315
  380.2 10.5 %collective-permute-start.45 = (f32[2,2,1,8,64]{4,3,2,1,0:T(8,128)S(1)}, f32[2,2,1,8,64]{4,3,2,1,0:T(8,128)S(1)}, u32[]{:S(2)}, u32[]{:S(2)}) collective-permute-start(f32[2,2,1,8,64]{4,3,2,1,0:T(8,128)S(1)} %get-tuple-element.194), channel_id=1, source_target_pairs={{4,0},{8,4},{12,8},{16,12},{20,16},{24,20},{28,24},{0,28},{5,1},{9... | collective-permute-start | bytes 24584 | tf_op jit(solution)/shard_map/ppermute | solution.py:29
  392.1 5.5 collective-permute-start.46
  405.4 10.9 %collective-permute-start.36 = (f32[2,1,16,128]{2,3,1,0:T(8,128)S(1)}, f32[2,1,16,128]{2,3,1,0:T(8,128)S(1)}, u32[]{:S(2)}, u32[]{:S(2)}) collective-permute-start(f32[2,1,16,128]{2,3,1,0:T(8,128)S(1)} %get-tuple-element.87), channel_id=1, source_target_pairs={{4,0},{8,4},{12,8},{16,12},{20,16},{24,20},{28,24},{0,28},{5,1},{9... | collective-permute-start | bytes 49160 | tf_op jit(solution)/shard_map/ppermute | solution.py:29
  430.8 4.8 collective-permute-start.37
  447.7 10.7 %collective-permute-start.49 = (f32[2,1,16,128]{2,3,1,0:T(8,128)S(1)}, f32[2,1,16,128]{2,3,1,0:T(8,128)S(1)}, u32[]{:S(2)}, u32[]{:S(2)}) collective-permute-start(f32[2,1,16,128]{2,3,1,0:T(8,128)S(1)} %get-tuple-element.81), channel_id=1, source_target_pairs={{4,0},{8,4},{12,8},{16,12},{20,16},{24,20},{28,24},{0,28},{5,1},{9... | collective-permute-start | bytes 49160 | tf_op jit(solution)/shard_map/ppermute | solution.py:29
  469.9 5.5 reshape.316
  510.4 10.5 %collective-permute-start.53 = (f32[2,1,8,64]{3,2,1,0:T(8,128)S(1)}, f32[2,1,8,64]{3,2,1,0:T(8,128)S(1)}, u32[]{:S(2)}, u32[]{:S(2)}) collective-permute-start(f32[2,1,8,64]{3,2,1,0:T(8,128)S(1)} %get-tuple-element.224), channel_id=1, source_target_pairs={{4,0},{8,4},{12,8},{16,12},{20,16},{24,20},{28,24},{0,28},{5,1},{9... | collective-permute-start | bytes 12296 | tf_op jit(solution)/shard_map/ppermute | solution.py:29
  522.3 4.9 collective-permute-start.54
  529.4 4.5 collective-permute-done.55
  542.7 10.8 %collective-permute-start.62 = (f32[2,2,1,16,128]{4,3,2,1,0:T(8,128)S(1)}, f32[2,2,1,16,128]{4,3,2,1,0:T(8,128)S(1)}, u32[]{:S(2)}, u32[]{:S(2)}) collective-permute-start(f32[2,2,1,16,128]{4,3,2,1,0:T(8,128)S(1)} %get-tuple-element.127), channel_id=1, source_target_pairs={{4,0},{8,4},{12,8},{16,12},{20,16},{24,20},{28,24},{0,28},{5,1},{9... | collective-permute-start | bytes 98312 | tf_op jit(solution)/shard_map/ppermute | solution.py:29
  553.5 7.8 collective-permute-done.69
  563.2 10.5 %collective-permute-start.71 = (f32[2,1,8,64]{3,2,1,0:T(8,128)S(1)}, f32[2,1,8,64]{3,2,1,0:T(8,128)S(1)}, u32[]{:S(2)}, u32[]{:S(2)}) collective-permute-start(f32[2,1,8,64]{3,2,1,0:T(8,128)S(1)} %get-tuple-element.218), channel_id=1, source_target_pairs={{4,0},{8,4},{12,8},{16,12},{20,16},{24,20},{28,24},{0,28},{5,1},{9... | collective-permute-start | bytes 12296 | tf_op jit(solution)/shard_map/ppermute | solution.py:29
  597.1 11.0 %collective-permute-start.58 = (f32[2,1,16,128]{2,3,1,0:T(8,128)S(1)}, f32[2,1,16,128]{2,3,1,0:T(8,128)S(1)}, u32[]{:S(2)}, u32[]{:S(2)}) collective-permute-start(f32[2,1,16,128]{2,3,1,0:T(8,128)S(1)} %get-tuple-element.75), channel_id=1, source_target_pairs={{4,0},{8,4},{12,8},{16,12},{20,16},{24,20},{28,24},{0,28},{5,1},{9... | collective-permute-start | bytes 49160 | tf_op jit(solution)/shard_map/ppermute | solution.py:29
  608.1 5.5 reshape.323
  622.4 5.4 collective-permute-start.59
  637.5 5.5 reshape.324
  647.5 10.5 %collective-permute-start.75 = (f32[2,2,1,8,64]{4,3,2,1,0:T(8,128)S(1)}, f32[2,2,1,8,64]{4,3,2,1,0:T(8,128)S(1)}, u32[]{:S(2)}, u32[]{:S(2)}) collective-permute-start(f32[2,2,1,8,64]{4,3,2,1,0:T(8,128)S(1)} %get-tuple-element.180), channel_id=1, source_target_pairs={{4,0},{8,4},{12,8},{16,12},{20,16},{24,20},{28,24},{0,28},{5,1},{9... | collective-permute-start | bytes 24584 | tf_op jit(solution)/shard_map/ppermute | solution.py:29
  659.5 5.4 collective-permute-start.76
  672.7 11.1 %collective-permute-start.66 = (f32[2,1,16,128]{2,3,1,0:T(8,128)S(1)}, f32[2,1,16,128]{2,3,1,0:T(8,128)S(1)}, u32[]{:S(2)}, u32[]{:S(2)}) collective-permute-start(f32[2,1,16,128]{2,3,1,0:T(8,128)S(1)} %copy-done.64), channel_id=1, source_target_pairs={{4,0},{8,4},{12,8},{16,12},{20,16},{24,20},{28,24},{0,28},{5,1},{9... | collective-permute-start | bytes 49160 | tf_op jit(solution)/shard_map/ppermute | solution.py:29
  698.1 5.0 collective-permute-start.67
  714.7 10.8 %collective-permute-start.79 = (f32[2,1,16,128]{2,3,1,0:T(8,128)}, f32[2,1,16,128]{2,3,1,0:T(8,128)}, u32[]{:S(2)}, u32[]{:S(2)}) collective-permute-start(f32[2,1,16,128]{2,3,1,0:T(8,128)} %get-tuple-element.63), channel_id=1, source_target_pairs={{4,0},{8,4},{12,8},{16,12},{20,16},{24,20},{28,24},{0,28},{5,1},{9... | collective-permute-start | bytes 49160 | tf_op jit(solution)/shard_map/ppermute | solution.py:29
  734.9 5.5 reshape.325
  764.5 10.5 %collective-permute-start.83 = (f32[2,1,8,64]{3,2,1,0:T(8,128)S(1)}, f32[2,1,8,64]{3,2,1,0:T(8,128)S(1)}, u32[]{:S(2)}, u32[]{:S(2)}) collective-permute-start(f32[2,1,8,64]{3,2,1,0:T(8,128)S(1)} %get-tuple-element.212), channel_id=1, source_target_pairs={{4,0},{8,4},{12,8},{16,12},{20,16},{24,20},{28,24},{0,28},{5,1},{9... | collective-permute-start | bytes 12296 | tf_op jit(solution)/shard_map/ppermute | solution.py:29
  776.4 4.5 collective-permute-start.84
  782.8 4.7 collective-permute-done.85
  (652 shorter events, 411.9 us)
Async XLA Ops:
  1.0 64.6 %collective-permute-start = (f32[2,4,16,128]{2,3,1,0:T(8,128)S(1)}, f32[2,4,16,128]{2,3,1,0:T(8,128)}, u32[]{:S(2)}, u32[]{:S(2)}) collective-permute-start(f32[2,4,16,128]{2,3,1,0:T(8,128)S(1)} %bitcast.544), channel_id=1, source_target_pairs={{0,32},{32,64},{64,96},{96,128},{128,160},{160,192},{192,224},{224... | collective-permute-start | bytes 196616 | tf_op jit(solution)/shard_map/ppermute | solution.py:18
  11.8 30.4 %collective-permute-start.9 = (f32[2,2,8,64]{3,2,1,0:T(8,128)S(1)}, f32[2,2,8,64]{3,2,1,0:T(8,128)S(1)}, u32[]{:S(2)}, u32[]{:S(2)}) collective-permute-start(f32[2,2,8,64]{3,2,1,0:T(8,128)S(1)} %broadcast_multiply_fusion), channel_id=1, source_target_pairs={{0,32},{32,64},{64,96},{96,128},{128,160},{160,192},{192,224},{224... | collective-permute-start | bytes 24584 | tf_op jit(solution)/shard_map/ppermute | solution.py:18
  42.3 12.5 %collective-permute-start.10 = (f32[2,1,8,64]{3,2,1,0:T(8,128)S(1)}, f32[2,1,8,64]{3,2,1,0:T(8,128)S(1)}, u32[]{:S(2)}, u32[]{:S(2)}) collective-permute-start(f32[2,1,8,64]{3,2,1,0:T(8,128)S(1)} %get-tuple-element.241), channel_id=1, source_target_pairs={{0,4},{4,8},{8,12},{12,16},{16,20},{20,24},{24,28},{28,0},{1,5},{5... | collective-permute-start | bytes 12296 | tf_op jit(solution)/shard_map/ppermute | solution.py:28
  67.9 21.0 %collective-permute-start.1 = (f32[2,1,16,128]{2,3,1,0:T(8,128)S(1)}, f32[2,1,16,128]{2,3,1,0:T(8,128)S(1)}, u32[]{:S(2)}, u32[]{:S(2)}) collective-permute-start(f32[2,1,16,128]{2,3,1,0:T(8,128)S(1)} %get-tuple-element.110), channel_id=1, source_target_pairs={{0,4},{4,8},{8,12},{12,16},{16,20},{20,24},{24,28},{28,0},{1,5},{5... | collective-permute-start | bytes 49160 | tf_op jit(solution)/shard_map/ppermute | solution.py:28
  69.8 19.1 %collective-permute-start.2 = (f32[2,1,16,128]{2,3,1,0:T(8,128)S(1)}, f32[2,1,16,128]{2,3,1,0:T(8,128)S(1)}, u32[]{:S(2)}, u32[]{:S(2)}) collective-permute-start(f32[2,1,16,128]{2,3,1,0:T(8,128)S(1)} %get-tuple-element.111), channel_id=1, source_target_pairs={{4,0},{8,4},{12,8},{16,12},{20,16},{24,20},{28,24},{0,28},{5,1},{9... | collective-permute-start | bytes 49160 | tf_op jit(solution)/shard_map/ppermute | solution.py:29
  114.1 12.5 %collective-permute-start.14 = (f32[2,2,1,8,64]{4,3,2,1,0:T(8,128)S(1)}, f32[2,2,1,8,64]{4,3,2,1,0:T(8,128)S(1)}, u32[]{:S(2)}, u32[]{:S(2)}) collective-permute-start(f32[2,2,1,8,64]{4,3,2,1,0:T(8,128)S(1)} %get-tuple-element.205), channel_id=1, source_target_pairs={{0,4},{4,8},{8,12},{12,16},{16,20},{20,24},{24,28},{28,0},{1,5},{5... | collective-permute-start | bytes 24584 | tf_op jit(solution)/shard_map/ppermute | solution.py:28
  116.0 12.0 %collective-permute-start.15 = (f32[2,2,1,8,64]{4,3,2,1,0:T(8,128)S(1)}, f32[2,2,1,8,64]{4,3,2,1,0:T(8,128)S(1)}, u32[]{:S(2)}, u32[]{:S(2)}) collective-permute-start(f32[2,2,1,8,64]{4,3,2,1,0:T(8,128)S(1)} %get-tuple-element.206), channel_id=1, source_target_pairs={{4,0},{8,4},{12,8},{16,12},{20,16},{24,20},{28,24},{0,28},{5,1},{9... | collective-permute-start | bytes 24584 | tf_op jit(solution)/shard_map/ppermute | solution.py:29
  128.0 29.8 %collective-permute-start.16 = (f32[2,2,4,1,64]{4,3,2,1,0:T(1,128)S(1)}, f32[2,2,4,1,64]{4,3,2,1,0:T(1,128)S(1)}, u32[]{:S(2)}, u32[]{:S(2)}) collective-permute-start(f32[2,2,4,1,64]{4,3,2,1,0:T(1,128)S(1)} %get-tuple-element.158), channel_id=1, source_target_pairs={{0,1},{1,2},{2,3},{3,0},{4,5},{5,6},{6,7},{7,4},{8,9},{9,10},{10,1... | collective-permute-start | bytes 12296 | tf_op jit(solution)/shard_map/ppermute | solution.py:28
  132.4 25.5 %collective-permute-start.17 = (f32[2,2,4,1,64]{4,3,2,1,0:T(1,128)S(1)}, f32[2,2,4,1,64]{4,3,2,1,0:T(1,128)S(1)}, u32[]{:S(2)}, u32[]{:S(2)}) collective-permute-start(f32[2,2,4,1,64]{4,3,2,1,0:T(1,128)S(1)} %get-tuple-element.159), channel_id=1, source_target_pairs={{1,0},{2,1},{3,2},{0,3},{5,4},{6,5},{7,6},{4,7},{9,8},{10,9},{11,1... | collective-permute-start | bytes 12296 | tf_op jit(solution)/shard_map/ppermute | solution.py:29
  138.9 19.6 %collective-permute-start.5 = (f32[2,1,16,128]{2,3,1,0:T(8,128)S(1)}, f32[2,1,16,128]{2,3,1,0:T(8,128)S(1)}, u32[]{:S(2)}, u32[]{:S(2)}) collective-permute-start(f32[2,1,16,128]{2,3,1,0:T(8,128)S(1)} %get-tuple-element.104), channel_id=1, source_target_pairs={{0,4},{4,8},{8,12},{12,16},{16,20},{20,24},{24,28},{28,0},{1,5},{5... | collective-permute-start | bytes 49160 | tf_op jit(solution)/shard_map/ppermute | solution.py:28
  140.9 17.7 %collective-permute-start.6 = (f32[2,1,16,128]{2,3,1,0:T(8,128)S(1)}, f32[2,1,16,128]{2,3,1,0:T(8,128)S(1)}, u32[]{:S(2)}, u32[]{:S(2)}) collective-permute-start(f32[2,1,16,128]{2,3,1,0:T(8,128)S(1)} %get-tuple-element.105), channel_id=1, source_target_pairs={{4,0},{8,4},{12,8},{16,12},{20,16},{24,20},{28,24},{0,28},{5,1},{9... | collective-permute-start | bytes 49160 | tf_op jit(solution)/shard_map/ppermute | solution.py:29
  163.3 12.0 %collective-permute-start.8 = (f32[2,6,1,128]{3,0,2,1:T(2,128)}, f32[2,6,1,128]{3,0,2,1:T(2,128)}, u32[]{:S(2)}, u32[]{:S(2)}) collective-permute-start(f32[2,6,1,128]{3,0,2,1:T(2,128)} %copy.427), channel_id=1, source_target_pairs={{1,0},{2,1},{3,2},{0,3},{5,4},{6,5},{7,6},{4,7},{9,8},{10,9},{11,1... | collective-permute-start | bytes 18440 | tf_op jit(solution)/shard_map/ppermute | solution.py:29
  183.7 31.9 %collective-permute-start.18 = (f32[2,1,16,128]{2,3,1,0:T(8,128)}, f32[2,1,16,128]{2,3,1,0:T(8,128)S(1)}, u32[]{:S(2)}, u32[]{:S(2)}) collective-permute-start(f32[2,1,16,128]{2,3,1,0:T(8,128)} %get-tuple-element.98), channel_id=1, source_target_pairs={{0,4},{4,8},{8,12},{12,16},{16,20},{20,24},{24,28},{28,0},{1,5},{5... | collective-permute-start | bytes 49160 | tf_op jit(solution)/shard_map/ppermute | solution.py:28
  185.6 30.0 %collective-permute-start.19 = (f32[2,1,16,128]{2,3,1,0:T(8,128)}, f32[2,1,16,128]{2,3,1,0:T(8,128)S(1)}, u32[]{:S(2)}, u32[]{:S(2)}) collective-permute-start(f32[2,1,16,128]{2,3,1,0:T(8,128)} %get-tuple-element.99), channel_id=1, source_target_pairs={{4,0},{8,4},{12,8},{16,12},{20,16},{24,20},{28,24},{0,28},{5,1},{9... | collective-permute-start | bytes 49160 | tf_op jit(solution)/shard_map/ppermute | solution.py:29
  220.4 12.0 %collective-permute-start.21 = (f32[2,6,1,128]{3,0,2,1:T(2,128)}, f32[2,6,1,128]{3,0,2,1:T(2,128)}, u32[]{:S(2)}, u32[]{:S(2)}) collective-permute-start(f32[2,6,1,128]{3,0,2,1:T(2,128)} %copy.452), channel_id=1, source_target_pairs={{1,0},{2,1},{3,2},{0,3},{5,4},{6,5},{7,6},{4,7},{9,8},{10,9},{11,1... | collective-permute-start | bytes 18440 | tf_op jit(solution)/shard_map/ppermute | solution.py:29
  245.4 13.0 %collective-permute-start.22 = (f32[2,1,8,64]{3,2,1,0:T(8,128)S(1)}, f32[2,1,8,64]{3,2,1,0:T(8,128)S(1)}, u32[]{:S(2)}, u32[]{:S(2)}) collective-permute-start(f32[2,1,8,64]{3,2,1,0:T(8,128)S(1)} %get-tuple-element.235), channel_id=1, source_target_pairs={{0,4},{4,8},{8,12},{12,16},{16,20},{20,24},{24,28},{28,0},{1,5},{5... | collective-permute-start | bytes 12296 | tf_op jit(solution)/shard_map/ppermute | solution.py:28
  270.0 20.8 %collective-permute-start.39 = (f32[2,2,8,64]{3,2,1,0:T(8,128)S(1)}, f32[2,2,8,64]{3,2,1,0:T(8,128)S(1)}, u32[]{:S(2)}, u32[]{:S(2)}) collective-permute-start(f32[2,2,8,64]{3,2,1,0:T(8,128)S(1)} %get-tuple-element.18), channel_id=1, source_target_pairs={{0,32},{32,64},{64,96},{96,128},{128,160},{160,192},{192,224},{224... | collective-permute-start | bytes 24584 | tf_op jit(solution)/shard_map/ppermute | solution.py:18
  272.0 52.3 %collective-permute-start.26 = (f32[2,4,16,128]{2,3,1,0:T(8,128)S(1)}, f32[2,4,16,128]{2,3,1,0:T(8,128)}, u32[]{:S(2)}, u32[]{:S(2)}) collective-permute-start(f32[2,4,16,128]{2,3,1,0:T(8,128)S(1)} %add.756), channel_id=1, source_target_pairs={{0,32},{32,64},{64,96},{96,128},{128,160},{160,192},{192,224},{224... | collective-permute-start | bytes 196616 | tf_op jit(solution)/shard_map/ppermute | solution.py:18
  277.9 35.4 %collective-permute-start.31 = (f32[2,2,1,16,128]{4,3,2,1,0:T(8,128)S(1)}, f32[2,2,1,16,128]{4,3,2,1,0:T(8,128)S(1)}, u32[]{:S(2)}, u32[]{:S(2)}) collective-permute-start(f32[2,2,1,16,128]{4,3,2,1,0:T(8,128)S(1)} %get-tuple-element.134), channel_id=1, source_target_pairs={{0,4},{4,8},{8,12},{12,16},{16,20},{20,24},{24,28},{28,0},{1,5},{5... | collective-permute-start | bytes 98312 | tf_op jit(solution)/shard_map/ppermute | solution.py:28
  279.9 33.5 %collective-permute-start.32 = (f32[2,2,1,16,128]{4,3,2,1,0:T(8,128)S(1)}, f32[2,2,1,16,128]{4,3,2,1,0:T(8,128)S(1)}, u32[]{:S(2)}, u32[]{:S(2)}) collective-permute-start(f32[2,2,1,16,128]{4,3,2,1,0:T(8,128)S(1)} %get-tuple-element.135), channel_id=1, source_target_pairs={{4,0},{8,4},{12,8},{16,12},{20,16},{24,20},{28,24},{0,28},{5,1},{9... | collective-permute-start | bytes 98312 | tf_op jit(solution)/shard_map/ppermute | solution.py:29
  290.8 12.5 %collective-permute-start.40 = (f32[2,1,8,64]{3,2,1,0:T(8,128)S(1)}, f32[2,1,8,64]{3,2,1,0:T(8,128)S(1)}, u32[]{:S(2)}, u32[]{:S(2)}) collective-permute-start(f32[2,1,8,64]{3,2,1,0:T(8,128)S(1)} %get-tuple-element.229), channel_id=1, source_target_pairs={{0,4},{4,8},{8,12},{12,16},{16,20},{20,24},{24,28},{28,0},{1,5},{5... | collective-permute-start | bytes 12296 | tf_op jit(solution)/shard_map/ppermute | solution.py:28
  327.2 21.8 %collective-permute-start.27 = (f32[2,1,16,128]{2,3,1,0:T(8,128)S(1)}, f32[2,1,16,128]{2,3,1,0:T(8,128)S(1)}, u32[]{:S(2)}, u32[]{:S(2)}) collective-permute-start(f32[2,1,16,128]{2,3,1,0:T(8,128)S(1)} %get-tuple-element.92), channel_id=1, source_target_pairs={{0,4},{4,8},{8,12},{12,16},{16,20},{20,24},{24,28},{28,0},{1,5},{5... | collective-permute-start | bytes 49160 | tf_op jit(solution)/shard_map/ppermute | solution.py:28
  329.1 19.9 %collective-permute-start.28 = (f32[2,1,16,128]{2,3,1,0:T(8,128)S(1)}, f32[2,1,16,128]{2,3,1,0:T(8,128)S(1)}, u32[]{:S(2)}, u32[]{:S(2)}) collective-permute-start(f32[2,1,16,128]{2,3,1,0:T(8,128)S(1)} %get-tuple-element.93), channel_id=1, source_target_pairs={{4,0},{8,4},{12,8},{16,12},{20,16},{24,20},{28,24},{0,28},{5,1},{9... | collective-permute-start | bytes 49160 | tf_op jit(solution)/shard_map/ppermute | solution.py:29
  378.2 12.5 %collective-permute-start.44 = (f32[2,2,1,8,64]{4,3,2,1,0:T(8,128)S(1)}, f32[2,2,1,8,64]{4,3,2,1,0:T(8,128)S(1)}, u32[]{:S(2)}, u32[]{:S(2)}) collective-permute-start(f32[2,2,1,8,64]{4,3,2,1,0:T(8,128)S(1)} %get-tuple-element.193), channel_id=1, source_target_pairs={{0,4},{4,8},{8,12},{12,16},{16,20},{20,24},{24,28},{28,0},{1,5},{5... | collective-permute-start | bytes 24584 | tf_op jit(solution)/shard_map/ppermute | solution.py:28
  380.2 12.0 %collective-permute-start.45 = (f32[2,2,1,8,64]{4,3,2,1,0:T(8,128)S(1)}, f32[2,2,1,8,64]{4,3,2,1,0:T(8,128)S(1)}, u32[]{:S(2)}, u32[]{:S(2)}) collective-permute-start(f32[2,2,1,8,64]{4,3,2,1,0:T(8,128)S(1)} %get-tuple-element.194), channel_id=1, source_target_pairs={{4,0},{8,4},{12,8},{16,12},{20,16},{24,20},{28,24},{0,28},{5,1},{9... | collective-permute-start | bytes 24584 | tf_op jit(solution)/shard_map/ppermute | solution.py:29
  392.1 30.3 %collective-permute-start.46 = (f32[2,2,4,1,64]{4,3,2,1,0:T(1,128)S(1)}, f32[2,2,4,1,64]{4,3,2,1,0:T(1,128)S(1)}, u32[]{:S(2)}, u32[]{:S(2)}) collective-permute-start(f32[2,2,4,1,64]{4,3,2,1,0:T(1,128)S(1)} %get-tuple-element.148), channel_id=1, source_target_pairs={{0,1},{1,2},{2,3},{3,0},{4,5},{5,6},{6,7},{7,4},{8,9},{9,10},{10,1... | collective-permute-start | bytes 12296 | tf_op jit(solution)/shard_map/ppermute | solution.py:28
  397.7 24.7 %collective-permute-start.47 = (f32[2,2,4,1,64]{4,3,2,1,0:T(1,128)S(1)}, f32[2,2,4,1,64]{4,3,2,1,0:T(1,128)S(1)}, u32[]{:S(2)}, u32[]{:S(2)}) collective-permute-start(f32[2,2,4,1,64]{4,3,2,1,0:T(1,128)S(1)} %get-tuple-element.149), channel_id=1, source_target_pairs={{1,0},{2,1},{3,2},{0,3},{5,4},{6,5},{7,6},{4,7},{9,8},{10,9},{11,1... | collective-permute-start | bytes 12296 | tf_op jit(solution)/shard_map/ppermute | solution.py:29
  403.5 19.7 %collective-permute-start.35 = (f32[2,1,16,128]{2,3,1,0:T(8,128)S(1)}, f32[2,1,16,128]{2,3,1,0:T(8,128)S(1)}, u32[]{:S(2)}, u32[]{:S(2)}) collective-permute-start(f32[2,1,16,128]{2,3,1,0:T(8,128)S(1)} %get-tuple-element.86), channel_id=1, source_target_pairs={{0,4},{4,8},{8,12},{12,16},{16,20},{20,24},{24,28},{28,0},{1,5},{5... | collective-permute-start | bytes 49160 | tf_op jit(solution)/shard_map/ppermute | solution.py:28
  405.4 17.7 %collective-permute-start.36 = (f32[2,1,16,128]{2,3,1,0:T(8,128)S(1)}, f32[2,1,16,128]{2,3,1,0:T(8,128)S(1)}, u32[]{:S(2)}, u32[]{:S(2)}) collective-permute-start(f32[2,1,16,128]{2,3,1,0:T(8,128)S(1)} %get-tuple-element.87), channel_id=1, source_target_pairs={{4,0},{8,4},{12,8},{16,12},{20,16},{24,20},{28,24},{0,28},{5,1},{9... | collective-permute-start | bytes 49160 | tf_op jit(solution)/shard_map/ppermute | solution.py:29
  445.8 32.8 %collective-permute-start.48 = (f32[2,1,16,128]{2,3,1,0:T(8,128)S(1)}, f32[2,1,16,128]{2,3,1,0:T(8,128)S(1)}, u32[]{:S(2)}, u32[]{:S(2)}) collective-permute-start(f32[2,1,16,128]{2,3,1,0:T(8,128)S(1)} %get-tuple-element.80), channel_id=1, source_target_pairs={{0,4},{4,8},{8,12},{12,16},{16,20},{20,24},{24,28},{28,0},{1,5},{5... | collective-permute-start | bytes 49160 | tf_op jit(solution)/shard_map/ppermute | solution.py:28
  447.7 30.9 %collective-permute-start.49 = (f32[2,1,16,128]{2,3,1,0:T(8,128)S(1)}, f32[2,1,16,128]{2,3,1,0:T(8,128)S(1)}, u32[]{:S(2)}, u32[]{:S(2)}) collective-permute-start(f32[2,1,16,128]{2,3,1,0:T(8,128)S(1)} %get-tuple-element.81), channel_id=1, source_target_pairs={{4,0},{8,4},{12,8},{16,12},{20,16},{24,20},{28,24},{0,28},{5,1},{9... | collective-permute-start | bytes 49160 | tf_op jit(solution)/shard_map/ppermute | solution.py:29
  508.5 13.0 %collective-permute-start.52 = (f32[2,1,8,64]{3,2,1,0:T(8,128)S(1)}, f32[2,1,8,64]{3,2,1,0:T(8,128)S(1)}, u32[]{:S(2)}, u32[]{:S(2)}) collective-permute-start(f32[2,1,8,64]{3,2,1,0:T(8,128)S(1)} %get-tuple-element.223), channel_id=1, source_target_pairs={{0,4},{4,8},{8,12},{12,16},{16,20},{20,24},{24,28},{28,0},{1,5},{5... | collective-permute-start | bytes 12296 | tf_op jit(solution)/shard_map/ppermute | solution.py:28
  536.8 24.5 %collective-permute-start.69 = (f32[2,2,8,64]{3,2,1,0:T(8,128)S(1)}, f32[2,2,8,64]{3,2,1,0:T(8,128)S(1)}, u32[]{:S(2)}, u32[]{:S(2)}) collective-permute-start(f32[2,2,8,64]{3,2,1,0:T(8,128)S(1)} %get-tuple-element.14), channel_id=1, source_target_pairs={{0,32},{32,64},{64,96},{96,128},{128,160},{160,192},{192,224},{224... | collective-permute-start | bytes 24584 | tf_op jit(solution)/shard_map/ppermute | solution.py:18
  538.7 55.1 %collective-permute-start.56 = (f32[2,4,16,128]{2,3,1,0:T(8,128)}, f32[2,4,16,128]{2,3,1,0:T(8,128)S(1)}, u32[]{:S(2)}, u32[]{:S(2)}) collective-permute-start(f32[2,4,16,128]{2,3,1,0:T(8,128)} %add.830), channel_id=1, source_target_pairs={{0,32},{32,64},{64,96},{96,128},{128,160},{160,192},{192,224},{224... | collective-permute-start | bytes 196616 | tf_op jit(solution)/shard_map/ppermute | solution.py:18
  540.7 43.1 %collective-permute-start.61 = (f32[2,2,1,16,128]{4,3,2,1,0:T(8,128)S(1)}, f32[2,2,1,16,128]{4,3,2,1,0:T(8,128)S(1)}, u32[]{:S(2)}, u32[]{:S(2)}) collective-permute-start(f32[2,2,1,16,128]{4,3,2,1,0:T(8,128)S(1)} %get-tuple-element.126), channel_id=1, source_target_pairs={{0,4},{4,8},{8,12},{12,16},{16,20},{20,24},{24,28},{28,0},{1,5},{5... | collective-permute-start | bytes 98312 | tf_op jit(solution)/shard_map/ppermute | solution.py:28
  542.7 41.2 %collective-permute-start.62 = (f32[2,2,1,16,128]{4,3,2,1,0:T(8,128)S(1)}, f32[2,2,1,16,128]{4,3,2,1,0:T(8,128)S(1)}, u32[]{:S(2)}, u32[]{:S(2)}) collective-permute-start(f32[2,2,1,16,128]{4,3,2,1,0:T(8,128)S(1)} %get-tuple-element.127), channel_id=1, source_target_pairs={{4,0},{8,4},{12,8},{16,12},{20,16},{24,20},{28,24},{0,28},{5,1},{9... | collective-permute-start | bytes 98312 | tf_op jit(solution)/shard_map/ppermute | solution.py:29
  561.3 12.5 %collective-permute-start.70 = (f32[2,1,8,64]{3,2,1,0:T(8,128)S(1)}, f32[2,1,8,64]{3,2,1,0:T(8,128)S(1)}, u32[]{:S(2)}, u32[]{:S(2)}) collective-permute-start(f32[2,1,8,64]{3,2,1,0:T(8,128)S(1)} %get-tuple-element.217), channel_id=1, source_target_pairs={{0,4},{4,8},{8,12},{12,16},{16,20},{20,24},{24,28},{28,0},{1,5},{5... | collective-permute-start | bytes 12296 | tf_op jit(solution)/shard_map/ppermute | solution.py:28
  595.2 21.0 %collective-permute-start.57 = (f32[2,1,16,128]{2,3,1,0:T(8,128)S(1)}, f32[2,1,16,128]{2,3,1,0:T(8,128)S(1)}, u32[]{:S(2)}, u32[]{:S(2)}) collective-permute-start(f32[2,1,16,128]{2,3,1,0:T(8,128)S(1)} %get-tuple-element.74), channel_id=1, source_target_pairs={{0,4},{4,8},{8,12},{12,16},{16,20},{20,24},{24,28},{28,0},{1,5},{5... | collective-permute-start | bytes 49160 | tf_op jit(solution)/shard_map/ppermute | solution.py:28
  597.1 19.1 %collective-permute-start.58 = (f32[2,1,16,128]{2,3,1,0:T(8,128)S(1)}, f32[2,1,16,128]{2,3,1,0:T(8,128)S(1)}, u32[]{:S(2)}, u32[]{:S(2)}) collective-permute-start(f32[2,1,16,128]{2,3,1,0:T(8,128)S(1)} %get-tuple-element.75), channel_id=1, source_target_pairs={{4,0},{8,4},{12,8},{16,12},{20,16},{24,20},{28,24},{0,28},{5,1},{9... | collective-permute-start | bytes 49160 | tf_op jit(solution)/shard_map/ppermute | solution.py:29
  645.6 12.5 %collective-permute-start.74 = (f32[2,2,1,8,64]{4,3,2,1,0:T(8,128)S(1)}, f32[2,2,1,8,64]{4,3,2,1,0:T(8,128)S(1)}, u32[]{:S(2)}, u32[]{:S(2)}) collective-permute-start(f32[2,2,1,8,64]{4,3,2,1,0:T(8,128)S(1)} %get-tuple-element.179), channel_id=1, source_target_pairs={{0,4},{4,8},{8,12},{12,16},{16,20},{20,24},{24,28},{28,0},{1,5},{5... | collective-permute-start | bytes 24584 | tf_op jit(solution)/shard_map/ppermute | solution.py:28
  647.5 12.0 %collective-permute-start.75 = (f32[2,2,1,8,64]{4,3,2,1,0:T(8,128)S(1)}, f32[2,2,1,8,64]{4,3,2,1,0:T(8,128)S(1)}, u32[]{:S(2)}, u32[]{:S(2)}) collective-permute-start(f32[2,2,1,8,64]{4,3,2,1,0:T(8,128)S(1)} %get-tuple-element.180), channel_id=1, source_target_pairs={{4,0},{8,4},{12,8},{16,12},{20,16},{24,20},{28,24},{0,28},{5,1},{9... | collective-permute-start | bytes 24584 | tf_op jit(solution)/shard_map/ppermute | solution.py:29
  659.5 30.3 %collective-permute-start.76 = (f32[2,2,4,1,64]{4,3,2,1,0:T(1,128)S(1)}, f32[2,2,4,1,64]{4,3,2,1,0:T(1,128)S(1)}, u32[]{:S(2)}, u32[]{:S(2)}) collective-permute-start(f32[2,2,4,1,64]{4,3,2,1,0:T(1,128)S(1)} %get-tuple-element.140), channel_id=1, source_target_pairs={{0,1},{1,2},{2,3},{3,0},{4,5},{5,6},{6,7},{7,4},{8,9},{9,10},{10,1... | collective-permute-start | bytes 12296 | tf_op jit(solution)/shard_map/ppermute | solution.py:28
  664.9 24.9 %collective-permute-start.77 = (f32[2,2,4,1,64]{4,3,2,1,0:T(1,128)S(1)}, f32[2,2,4,1,64]{4,3,2,1,0:T(1,128)S(1)}, u32[]{:S(2)}, u32[]{:S(2)}) collective-permute-start(f32[2,2,4,1,64]{4,3,2,1,0:T(1,128)S(1)} %get-tuple-element.141), channel_id=1, source_target_pairs={{1,0},{2,1},{3,2},{0,3},{5,4},{6,5},{7,6},{4,7},{9,8},{10,9},{11,1... | collective-permute-start | bytes 12296 | tf_op jit(solution)/shard_map/ppermute | solution.py:29
  670.7 19.8 %collective-permute-start.65 = (f32[2,1,16,128]{2,3,1,0:T(8,128)S(1)}, f32[2,1,16,128]{2,3,1,0:T(8,128)S(1)}, u32[]{:S(2)}, u32[]{:S(2)}) collective-permute-start(f32[2,1,16,128]{2,3,1,0:T(8,128)S(1)} %copy-done.65), channel_id=1, source_target_pairs={{0,4},{4,8},{8,12},{12,16},{16,20},{20,24},{24,28},{28,0},{1,5},{5... | collective-permute-start | bytes 49160 | tf_op jit(solution)/shard_map/ppermute | solution.py:28
  672.7 17.9 %collective-permute-start.66 = (f32[2,1,16,128]{2,3,1,0:T(8,128)S(1)}, f32[2,1,16,128]{2,3,1,0:T(8,128)S(1)}, u32[]{:S(2)}, u32[]{:S(2)}) collective-permute-start(f32[2,1,16,128]{2,3,1,0:T(8,128)S(1)} %copy-done.64), channel_id=1, source_target_pairs={{4,0},{8,4},{12,8},{16,12},{20,16},{24,20},{28,24},{0,28},{5,1},{9... | collective-permute-start | bytes 49160 | tf_op jit(solution)/shard_map/ppermute | solution.py:29
  712.8 30.8 %collective-permute-start.78 = (f32[2,1,16,128]{2,3,1,0:T(8,128)}, f32[2,1,16,128]{2,3,1,0:T(8,128)S(1)}, u32[]{:S(2)}, u32[]{:S(2)}) collective-permute-start(f32[2,1,16,128]{2,3,1,0:T(8,128)} %get-tuple-element.62), channel_id=1, source_target_pairs={{0,4},{4,8},{8,12},{12,16},{16,20},{20,24},{24,28},{28,0},{1,5},{5... | collective-permute-start | bytes 49160 | tf_op jit(solution)/shard_map/ppermute | solution.py:28
  714.7 28.9 %collective-permute-start.79 = (f32[2,1,16,128]{2,3,1,0:T(8,128)}, f32[2,1,16,128]{2,3,1,0:T(8,128)}, u32[]{:S(2)}, u32[]{:S(2)}) collective-permute-start(f32[2,1,16,128]{2,3,1,0:T(8,128)} %get-tuple-element.63), channel_id=1, source_target_pairs={{4,0},{8,4},{12,8},{16,12},{20,16},{24,20},{28,24},{0,28},{5,1},{9... | collective-permute-start | bytes 49160 | tf_op jit(solution)/shard_map/ppermute | solution.py:29
  762.5 12.5 %collective-permute-start.82 = (f32[2,1,8,64]{3,2,1,0:T(8,128)S(1)}, f32[2,1,8,64]{3,2,1,0:T(8,128)S(1)}, u32[]{:S(2)}, u32[]{:S(2)}) collective-permute-start(f32[2,1,8,64]{3,2,1,0:T(8,128)S(1)} %get-tuple-element.211), channel_id=1, source_target_pairs={{0,4},{4,8},{8,12},{12,16},{16,20},{20,24},{24,28},{28,0},{1,5},{5... | collective-permute-start | bytes 12296 | tf_op jit(solution)/shard_map/ppermute | solution.py:28
  (121 other events, 1262.8 us)
where the time goes:
time: 801 us; the launch traced here: 789 us
  starting transfers between devices  419 us (52%)
  local copies, waits for them, and re-layouts  257 us (32%)
  other arithmetic  67 us (8%)
  waiting for transfers between devices  43.3 us (5%)
    ppermute x40, starting transfers between devices, with_halo(): after = lax.ppermute(first, axis, down)  265 us
    ppermute x40, starting transfers between devices, with_halo(): before = lax.ppermute(last, axis, up)  125 us
    another operation x38, local copies, waits for them, and re-layouts, source_terms(): return jnp.stack([rate_u, rate_v], axis=-4)  79.5 us
    reshape x12, local copies, waits for them, and re-layouts, restrict(): grid_field.reshape(leading + (size_x // 2, 2, size_y // 2, 2, size_z // 2...  59.2 us
    ppermute x40, waiting for transfers between devices, with_halo(): after = lax.ppermute(first, axis, down)  32.1 us
    reduce_sum x16, other arithmetic, restrict(): return 0.125 * jnp.sum(blocks, axis=(-5, -3, -1))  30.5 us
    ppermute x6, starting transfers between devices, from_behind(): lax.ppermute(value, axis, [(source, source + steps) for source in range(f...  29.6 us
    slice x33, local copies, waits for them, and re-layouts, with_halo(): last = lax.slice_in_dim(shard, length - width, length, axis=dim)  27.9 us
  transfers between devices with their start and end apart: 86, of which 23 were waited for; matrix products, arithmetic and copies ran while one was open for 22% of the time, Pallas kernels for 0%

commit v1 on v0

v1 whole, which is shorter than its diff:
```python
import functools

import jax
import jax.numpy as jnp
from jax import lax
from jax.experimental import pallas as pl
from jax.experimental.pallas import tpu as pltpu
from jax.sharding import PartitionSpec as P

ITERS = 3
DIFF = (0.2, 0.1)
HALF_STEP = 0.5
WEIGHTS = ((5.0 / 24.0, 8.0 / 24.0, -1.0 / 24.0), (-1.0 / 24.0, 8.0 / 24.0, 5.0 / 24.0))

PLANES, ROWS, LANES = 4, 16, 128
TALL, LOW, WINDOW, OWN = 40, 8, 24, 12
HALO = 3
N_SEMS = 112


def kernel(dims, init_ref, guess_ref, feed_ref, kill_ref, out_ref,
           s_buf, c_buf, u_buf, w_buf, v1_buf, v2_buf, fk_buf, g0_buf, a0_buf, a1_buf, q_buf, o_buf,
           send_sem, recv_sem):
    nt, ng, nx = dims
    chips = ng // 2
    blocks = nt // ng
    n, g, y = lax.axis_index("tm"), lax.axis_index("gy"), lax.axis_index("gx")

    def home_of(slice_at, tile):
        return slice_at, tile

    def role_of(slice_at, tile):
        return 2 * blocks * (tile // 2) + 2 * (slice_at // ng) + tile % 2, slice_at % ng

    def device(place, column):
        return {"tm": place[0], "gy": place[1], "gx": column}

    def is_me(place):
        return jnp.logical_and(place[0] == n, place[1] == g)

    across, block, core = n // (2 * blocks), (n // 2) % blocks, n % 2
    t = 2 * across + core
    m = ng * block + g

    s_to = role_of((n + 1) % nt, g)
    s_from = home_of((m + nt - 1) % nt, t)
    fk_to = role_of((g + nt - ng // 2 + ng * block + 2 * ((across + chips - g // 2) % chips) + core) % nt, g)
    fk_at = (m - t + ng // 2 + nt) % nt
    fk_from = (2 * blocks * ((t // 2 + (fk_at % ng) // 2) % chips) + 2 * (fk_at // ng) + fk_at % 2, t)
    out_to = home_of(m, t)
    out_from = role_of(n, g)
    later, earlier = role_of((m + 1) % nt, t), role_of((m + nt - 1) % nt, t)
    sides = [(dx, dy) for dx in (-1, 0, 1) for dy in (-1, 0, 1) if (dx, dy) != (0, 0)]
    faces = [(dx, dy) for dx, dy in sides if dx == 0 or dy == 0]

    def neighbour(dx, dy):
        return device(role_of(m, (t + dx + ng) % ng), (y + dy + nx) % nx)

    barrier = pltpu.get_barrier_semaphore()
    partners = [device(place, y) for place in (s_from, fk_from, out_from, earlier, later)]
    partners += [neighbour(dx, dy) for dx, dy in sides]
    for partner in partners:
        pl.semaphore_signal(barrier, inc=1, device_id=partner, device_id_type=pl.DeviceIdType.MESH)
    pl.semaphore_wait(barrier, len(partners))

    used = [0]
    started = []

    def remote(src, dst, where):
        index = used[0]
        used[0] += 1
        return pltpu.make_async_remote_copy(
            src_ref=src, dst_ref=dst, send_sem=send_sem.at[index], recv_sem=recv_sem.at[index],
            device_id=where, device_id_type=pl.DeviceIdType.MESH), index

    def move(src, dst, place, column, when=None):
        copy, index = remote(src, dst, device(place, column))
        local = pltpu.make_async_copy(src, dst, recv_sem.at[index])
        away = jnp.logical_not(is_me(place))
        if when is not None:
            here = jnp.logical_and(when, is_me(place))
            away = jnp.logical_and(when, away)
        else:
            here = is_me(place)

        @pl.when(away)
        def _():
            copy.start()

        @pl.when(here)
        def _():
            local.start()

        started.append((copy, away))
        return copy

    def halo_piece(dx, dy, lead, width, own_x, count, width_x):
        if dx == 0:
            sx, tx = pl.ds(own_x, count), pl.ds(own_x, count)
        elif dx > 0:
            sx, tx = pl.ds(own_x + count - width_x, width_x), pl.ds(own_x - width_x, width_x)
        else:
            sx, tx = pl.ds(own_x, width_x), pl.ds(own_x + count, width_x)
        if dy == 0:
            sy, ty = pl.ds(OWN, ROWS), pl.ds(OWN, ROWS)
        elif dy > 0:
            sy, ty = pl.ds(OWN + ROWS - width, width), pl.ds(OWN - width, width)
        else:
            sy, ty = pl.ds(OWN, width), pl.ds(OWN + ROWS, width)
        return (lead, sx, sy), (lead, tx, ty)

    def exchange(buf, fields, where, width, own_x, count, width_x):
        copies = []
        for dx, dy in where:
            src, dst = halo_piece(dx, dy, pl.ds(0, fields), width, own_x, count, width_x)
            copy, _ = remote(buf.at[src], buf.at[dst], neighbour(dx, dy))
            copy.start()
            started.append((copy, None))
            copies.append(copy)
        return copies

    def arrive(copies):
        for copy in copies:
            copy.wait_recv()

    own = (pl.ds(0, 2), pl.ds(HALO, PLANES), pl.ds(OWN, ROWS))
    own_c = (pl.ds(0, 2), pl.ds(1, 2), pl.ds(OWN, ROWS))

    fk_own = (pl.ds(2, PLANES), pl.ds(OWN, ROWS))
    feed_in = move(feed_ref, fk_buf.at[(0, *fk_own)], fk_to, y)
    kill_in = move(kill_ref, fk_buf.at[(1, *fk_own)], fk_to, y)
    first_s = s_buf.at[0]
    last_home = n == nt - 1
    mark = used[0]
    s_in = move(guess_ref.at[0], first_s.at[own], s_to, y, jnp.logical_not(last_home))
    used[0] = mark
    move(init_ref, first_s.at[own], s_to, y, last_home)

    row = lax.broadcasted_iota(jnp.int32, (WINDOW, LANES), 0)
    lane = lax.broadcasted_iota(jnp.int32, (WINDOW, LANES), 1)
    even_row, even_lane = row % 2 == 0, lane % 2 == 0

    def rows(by=0):
        return pl.ds(LOW + by, WINDOW)

    def turn(value, by, axis):
        size = value.shape[axis]
        return pltpu.roll(value, by % size, axis % value.ndim)

    def source(lap_u, lap_v, u, v, feed, both):
        reaction = u * v * v
        return lap_u - reaction + feed * (1.0 - u), lap_v + reaction - both * v

    def fine_rates(buf, first, at, feed_at, count):
        laps, mids = [], []
        for field in range(2):
            f = first + field
            mid = buf[f, pl.ds(at, count), rows(), :]
            total = buf[f, pl.ds(at - 1, count), rows(), :] + buf[f, pl.ds(at + 1, count), rows(), :]
            total = total + buf[f, pl.ds(at, count), rows(-1), :] + buf[f, pl.ds(at, count), rows(1), :]
            total = total + turn(mid, 1, -1) + turn(mid, -1, -1)
            laps.append(DIFF[field] * (total - 6.0 * mid))
            mids.append(mid)
        feed = fk_buf[0, pl.ds(feed_at, count), rows(), :]
        both = fk_buf[2, pl.ds(feed_at, count), rows(), :]
        return mids, source(laps[0], laps[1], mids[0], mids[1], feed, both)

    def pair_sum(value):
        value = value + jnp.where(even_row, turn(value, -1, -2), turn(value, 1, -2))
        return value + jnp.where(even_lane, turn(value, -1, -1), turn(value, 1, -1))

    def restrict(first, second):
        return 0.125 * pair_sum(first + second)

    def coarse_rates(below, mid, above, feed, both):
        laps = []
        for field in range(2):
            total = below[field] + above[field] + turn(mid[field], 2, -2) + turn(mid[field], -2, -2)
            total = total + turn(mid[field], 2, -1) + turn(mid[field], -2, -1)
            laps.append((0.25 * DIFF[field]) * (total - 6.0 * mid[field]))
        return source(laps[0], laps[1], mid[0], mid[1], feed, both)

    arrive((feed_in, kill_in))
    fk_halo = exchange(fk_buf, 2, sides, 2, 2, PLANES, 2)
    arrive((s_in,))
    s_halo = exchange(first_s, 2, sides, HALO, HALO, PLANES, HALO)
    c_halo = []
    arrive(fk_halo)
    for p in range(8):
        fk_buf[2, p, rows(), :] = fk_buf[0, p, rows(), :] + fk_buf[1, p, rows(), :]
    coarse_feed = [restrict(fk_buf[0, 2 + 2 * p, rows(), :], fk_buf[0, 3 + 2 * p, rows(), :]) for p in range(2)]
    coarse_kill = [restrict(fk_buf[1, 2 + 2 * p, rows(), :], fk_buf[1, 3 + 2 * p, rows(), :]) for p in range(2)]
    coarse_both = [coarse_feed[p] + coarse_kill[p] for p in range(2)]

    for k in range(ITERS):
        s_now, c_now, w_now = s_buf.at[k], c_buf.at[k], w_buf.at[k]
        last = k == ITERS - 1
        if k > 0:
            u_old = u_buf.at[k - 1]
            arrive(u_halo)
            for p in range(0, 8, 2):
                _, one = fine_rates(u_old, 0, p + 1, p, 2)
                _, two = fine_rates(u_old, 2, p + 1, p, 2)
                for field in range(2):
                    zero = g0_buf[field, pl.ds(p, 2), rows(), :]
                    a0_buf[field, pl.ds(p, 2), rows(), :] = (
                        (WEIGHTS[0][0] - HALF_STEP) * zero + WEIGHTS[0][1] * one[field] + WEIGHTS[0][2] * two[field])
                    a1_buf[field, pl.ds(p, 2), rows(), :] = (
                        WEIGHTS[1][0] * zero + (WEIGHTS[1][1] - HALF_STEP) * one[field] + WEIGHTS[1][2] * two[field])
        arrive(s_halo)
        for p in range(0, 8, 2):
            mids, rates = fine_rates(s_now, 0, p + 1, p, 2)
            for field in range(2):
                node = mids[field] + HALF_STEP * rates[field]
                if k > 0:
                    node = node + a0_buf[field, pl.ds(p, 2), rows(), :]
                g0_buf[field, pl.ds(p, 2), rows(), :] = rates[field]
                v1_buf[field, pl.ds(p, 2), rows(), :] = node
        for p in range(0, 6, 2):
            mids, rates = fine_rates(v1_buf, 0, p + 1, p + 1, 2)
            for field in range(2):
                node = mids[field] + HALF_STEP * rates[field]
                if k > 0:
                    node = node + a1_buf[field, pl.ds(p + 1, 2), rows(), :]
                v2_buf[field, pl.ds(p, 2), rows(), :] = node
                q_buf[field, pl.ds(p, 2), rows(), :] = rates[field]
        rest_s = [[restrict(s_now[f, 1 + 2 * p, rows(), :], s_now[f, 2 + 2 * p, rows(), :]) for f in range(2)]
                  for p in range(4)]
        if k == 0:
            coarse = rest_s
            for p in range(2):
                for f in range(2):
                    c_now[f, 1 + p, rows(), :] = coarse[1 + p][f]
        else:
            arrive(c_halo)
            coarse = [[c_now[f, p, rows(), :] for f in range(2)] for p in range(4)]
        rest_v1 = [[restrict(v1_buf[f, 2 * p, rows(), :], v1_buf[f, 1 + 2 * p, rows(), :]) for f in range(2)]
                   for p in range(4)]
        integral = []
        w_one = []
        for p in range(2):
            _, two = fine_rates(v2_buf, 0, 2 * p + 1, 2 * p + 2, 2)
            sums = []
            for f in range(2):
                zero = g0_buf[f, pl.ds(2 + 2 * p, 2), rows(), :]
                one = q_buf[f, pl.ds(1 + 2 * p, 2), rows(), :]
                whole = [weight[0] * zero + weight[1] * one + weight[2] * two[f] for weight in WEIGHTS]
                sums.append([restrict(q[0], q[1]) for q in whole])
            integral.append(sums)
            rate_c = coarse_rates(coarse[p], coarse[p + 1], coarse[p + 2], coarse_feed[p], coarse_both[p])
            rate_s = coarse_rates(rest_s[p], rest_s[p + 1], rest_s[p + 2], coarse_feed[p], coarse_both[p])
            w_one.append([coarse[p + 1][f] + HALF_STEP * (rate_c[f] - rate_s[f]) + sums[f][0] for f in range(2)])
            for f in range(2):
                w_now[f, 1 + p, pl.ds(OWN, ROWS), :] = w_one[p][f][OWN - LOW : OWN - LOW + ROWS]
        w_halo = exchange(w_now, 2, faces, 2, 1, 2, 1)
        rest_v2 = [[restrict(v2_buf[f, 1 + 2 * p, rows(), :], v2_buf[f, 2 + 2 * p, rows(), :]) for f in range(2)]
                   for p in range(2)]
        rate_v1 = [coarse_rates(rest_v1[p], rest_v1[p + 1], rest_v1[p + 2], coarse_feed[p], coarse_both[p])
                   for p in range(2)]
        arrive(w_halo)
        coarse_w = [[w_now[f, p, rows(), :] for f in range(2)] for p in range(4)]
        for p in range(2):
            rate_w = coarse_rates(coarse_w[p], coarse_w[p + 1], coarse_w[p + 2], coarse_feed[p], coarse_both[p])
            for f in range(2):
                w_two = w_one[p][f] + HALF_STEP * (rate_w[f] - rate_v1[p][f]) + integral[p][f][1]
                up_one = w_one[p][f] - rest_v1[p + 1][f]
                up_two = w_two - rest_v2[p][f]
                keep = slice(OWN - LOW, OWN - LOW + ROWS)
                for q in range(2):
                    at = 2 * p + q
                    two = v2_buf[f, at + 1, rows(), :] + up_two
                    if last:
                        o_buf[f, at, :, :] = two[keep]
                    else:
                        one = v1_buf[f, at + 2, rows(), :] + up_one
                        u_buf[k, f, HALO + at, pl.ds(OWN, ROWS), :] = one[keep]
                        u_buf[k, 2 + f, HALO + at, pl.ds(OWN, ROWS), :] = two[keep]
                if not last:
                    w_buf[ITERS + k, f, 1 + p, pl.ds(OWN, ROWS), :] = w_two[keep]
        if not last:
            u_now, s_next, c_next = u_buf.at[k], s_buf.at[k + 1], c_buf.at[k + 1]
            shifted = []
            for src, dst, kept in (
                (u_now.at[(pl.ds(2, 2), *own[1:])], s_next.at[own], s_now.at[own]),
                (w_buf.at[(ITERS + k, *own_c)], c_next.at[own_c], c_now.at[own_c]),
            ):
                copy, index = remote(src, dst, device(later, y))
                stay = pltpu.make_async_copy(kept, dst, recv_sem.at[index])
                onward = m < nt - 1

                @pl.when(onward)
                def _(copy=copy):
                    copy.start()

                @pl.when(m == 0)
                def _(stay=stay):
                    stay.start()

                started.append((copy, onward))
                shifted.append(copy)
            u_halo = exchange(u_now, 4, sides, HALO, HALO, PLANES, HALO)
            arrive(shifted[:1])
            s_halo = exchange(s_next, 2, sides, HALO, HALO, PLANES, HALO)
            arrive(shifted[1:])
            c_halo = exchange(c_next, 2, faces, 2, 1, 2, 1)

    out_in = move(o_buf, out_ref.at[0], out_to, y)
    arrive((out_in,))
    for copy, when in started:
        if when is None:
            copy.wait_send()
        else:

            @pl.when(when)
            def _(copy=copy):
                copy.wait_send()

    assert used[0] <= N_SEMS


def solution(mesh):
    dims = (mesh.shape["tm"], mesh.shape["gy"], mesh.shape["gx"])

    def shards(initial_state, slice_guess, feed_rate, kill_rate):
        buffers = [
            (ITERS, 2, 10, TALL, LANES),
            (ITERS, 2, 4, TALL, LANES),
            (ITERS - 1, 4, 10, TALL, LANES),
            (2 * ITERS - 1, 2, 4, TALL, LANES),
            (2, 8, TALL, LANES),
            (2, 6, TALL, LANES),
            (3, 8, TALL, LANES),
            (2, 8, TALL, LANES),
            (2, 8, TALL, LANES),
            (2, 8, TALL, LANES),
            (2, 6, TALL, LANES),
            (2, PLANES, ROWS, LANES),
        ]
        return pl.pallas_call(
            functools.partial(kernel, dims),
            out_shape=jax.ShapeDtypeStruct((1, 2, PLANES, ROWS, LANES), jnp.float32),
            in_specs=[pl.BlockSpec(memory_space=pl.ANY)] * 4,
            out_specs=pl.BlockSpec(memory_space=pl.ANY),
            scratch_shapes=[pltpu.VMEM(shape, jnp.float32) for shape in buffers]
            + [pltpu.SemaphoreType.DMA((N_SEMS,)), pltpu.SemaphoreType.DMA((N_SEMS,))],
            compiler_params=pltpu.CompilerParams(collective_id=0, has_side_effects=True),
        )(initial_state, slice_guess, feed_rate, kill_rate)

    in_specs = (
        P(None, "gy", "gx", None),
        P("tm", None, "gy", "gx", None),
        P("gy", "gx", None),
        P("gy", "gx", None),
    )
    out_specs = P("tm", None, "gy", "gx", None)
    return jax.shard_map(shards, mesh=mesh, in_specs=in_specs, out_specs=out_specs, check_vma=False)
```

time: 801 us -> 72 us (0.09)
  the two profiles are of different devices: /device:TPU:30 before, /device:TPU:5 now
where the time goes in v1:
time: 72 us; the launch traced here: 71.9 us
  Pallas kernels  70.4 us (98%)
  local copies, waits for them, and re-layouts  1.47 us (2%)
    pallas_call x1, Pallas kernels, shards(): pl.pallas_call(functools.partial(kernel, dims), out_shape=jax.ShapeDtypeS...  70.4 us
    unnamed x1, local copies, waits for them, and re-layouts  1.47 us

profile of v1, /device:TPU:5, one launch (start us, length us, event | category | flops | bytes accessed | tf_op | source)
XLA Modules:
  0.0 71.9 jit_solution(14334498232088301939)
XLA Ops:
  0.0 70.4 %shard_map.46 = f32[1,2,4,16,128]{4,3,2,1,0:T(8,128)} custom-call(f32[2,4,16,128]{3,2,1,0:T(8,128)} %init_ref.1, f32[1,2,4,16,128]{4,3,2,1,0:T(8,128)} %guess_ref.1, f32[4,16,128]{2,1,0:T(8,128)} %feed_ref.1, f32[4,16,128]{2,1,0:T(8,128)} %kill_ref.1), custom_call_target="tpu_custom_call" | custom-call | tf_op jit(solution)/shard_map/pallas_call | solution.py:339
  70.4 1.5 %copy.6 = f32[1,2,4,16,128]{4,3,2,1,0:T(8,128)} copy(f32[1,2,4,16,128]{4,3,2,1,0:T(8,128)} %shard_map.46) | data formatting | bytes 131072

commit v2 on v1

v2 whole, which is shorter than its diff:
```python
import functools

import jax
import jax.numpy as jnp
from jax import lax
from jax.experimental import pallas as pl
from jax.experimental.pallas import tpu as pltpu
from jax.sharding import PartitionSpec as P

ITERS = 3
DIFF = (0.2, 0.1)
HALF_STEP = 0.5
WEIGHTS = ((5.0 / 24.0, 8.0 / 24.0, -1.0 / 24.0), (-1.0 / 24.0, 8.0 / 24.0, 5.0 / 24.0))

PLANES, ROWS, LANES = 4, 16, 128
TALL, LOW, WINDOW, OWN = 40, 8, 24, 12
HALO = 5
SHIFT = 2
N_SEMS = 128


def kernel(dims, init_ref, guess_ref, feed_ref, kill_ref, out_ref,
           s_buf, c_buf, u_buf, w_buf, v1_buf, v2_buf, fk_buf, g0_buf, g1_buf, a0_buf, a1_buf, o_buf,
           send_sem, recv_sem):
    nt, ng, nx = dims
    chips = ng // 2
    blocks = nt // ng
    n, g, y = lax.axis_index("tm"), lax.axis_index("gy"), lax.axis_index("gx")

    def home_of(slice_at, tile):
        return slice_at, tile

    def role_of(slice_at, tile):
        along = (slice_at + SHIFT) % nt
        turned = (tile + 2 * (slice_at // (2 * blocks))) % ng
        return 2 * blocks * (turned // 2) + 2 * (along // ng) + turned % 2, along % ng

    def device(place, column):
        return {"tm": place[0], "gy": place[1], "gx": column}

    def is_me(place):
        return jnp.logical_and(place[0] == n, place[1] == g)

    across, block, core = n // (2 * blocks), (n // 2) % blocks, n % 2
    along = ng * block + g
    m = (along + nt - SHIFT) % nt
    t = (2 * across + core + ng - 2 * (m // (2 * blocks))) % ng

    s_to = role_of((n + 1) % nt, g)
    s_from = home_of((m + nt - 1) % nt, t)
    fk_along = g + nt - ng // 2 + ng * block + 2 * ((across + chips - g // 2) % chips) + core
    fk_to = role_of((fk_along + nt - SHIFT) % nt, g)
    fk_at = (along - t + ng // 2 + nt) % nt
    fk_from = (2 * blocks * ((t // 2 + (fk_at % ng) // 2) % chips) + 2 * (fk_at // ng) + fk_at % 2, t)
    out_to = home_of(m, t)
    out_from = role_of(n, g)
    later, earlier = role_of((m + 1) % nt, t), role_of((m + nt - 1) % nt, t)
    near = [(dx, dy) for dx in (-1, 0, 1) for dy in (-1, 0, 1) if (dx, dy) != (0, 0)]
    wide = near + [(dx, dy) for dx in (-2, 2) for dy in (-1, 0, 1)]

    def neighbour(dx, dy):
        return device(role_of(m, (t + dx + ng) % ng), (y + dy + nx) % nx)

    barrier = pltpu.get_barrier_semaphore()
    partners = [device(place, y) for place in (s_from, fk_from, out_from, earlier, later)]
    partners += [neighbour(dx, dy) for dx, dy in wide]
    for partner in partners:
        pl.semaphore_signal(barrier, inc=1, device_id=partner, device_id_type=pl.DeviceIdType.MESH)
    pl.semaphore_wait(barrier, len(partners))

    used = [0]
    started = []

    def remote(src, dst, where):
        index = used[0]
        used[0] += 1
        return pltpu.make_async_remote_copy(
            src_ref=src, dst_ref=dst, send_sem=send_sem.at[index], recv_sem=recv_sem.at[index],
            device_id=where, device_id_type=pl.DeviceIdType.MESH), index

    def move(src, dst, place, column, when=None):
        copy, index = remote(src, dst, device(place, column))
        local = pltpu.make_async_copy(src, dst, recv_sem.at[index])
        away = jnp.logical_not(is_me(place))
        if when is not None:
            here = jnp.logical_and(when, is_me(place))
            away = jnp.logical_and(when, away)
        else:
            here = is_me(place)

        @pl.when(away)
        def _():
            copy.start()

        @pl.when(here)
        def _():
            local.start()

        started.append((copy, away))
        return copy

    def exchange(buf, fields, where, own_x, count, width_x, width_y):
        copies = []
        for dx, dy in where:
            planes = count if dx == 0 else min(count, width_x - count * (abs(dx) - 1))
            from_x = own_x + count - planes if dx > 0 else own_x
            to_x = from_x - dx * count
            rows_sent = ROWS if dy == 0 else width_y
            from_y = OWN + ROWS - rows_sent if dy > 0 else OWN
            to_y = from_y - dy * ROWS
            src = buf.at[pl.ds(0, fields), pl.ds(from_x, planes), pl.ds(from_y, rows_sent)]
            dst = buf.at[pl.ds(0, fields), pl.ds(to_x, planes), pl.ds(to_y, rows_sent)]
            copy, _ = remote(src, dst, neighbour(dx, dy))
            copy.start()
            started.append((copy, None))
            copies.append(copy)
        return copies

    def arrive(copies):
        for copy in copies:
            copy.wait_recv()

    own = (pl.ds(0, 2), pl.ds(HALO, PLANES), pl.ds(OWN, ROWS))
    own_c = (pl.ds(0, 2), pl.ds(2, 2), pl.ds(OWN, ROWS))

    fk_own = (pl.ds(4, PLANES), pl.ds(OWN, ROWS))
    first_s = s_buf.at[0]
    last_home = n == nt - 1
    mark = used[0]
    s_in = move(guess_ref.at[0], first_s.at[own], s_to, y, jnp.logical_not(last_home))
    used[0] = mark
    move(init_ref, first_s.at[own], s_to, y, last_home)
    feed_in = move(feed_ref, fk_buf.at[(0, *fk_own)], fk_to, y)
    kill_in = move(kill_ref, fk_buf.at[(1, *fk_own)], fk_to, y)

    row = lax.broadcasted_iota(jnp.int32, (WINDOW, LANES), 0)
    lane = lax.broadcasted_iota(jnp.int32, (WINDOW, LANES), 1)
    even_row, even_lane = row % 2 == 0, lane % 2 == 0

    def rows(by=0):
        return pl.ds(LOW + by, WINDOW)

    def turn(value, by, axis):
        size = value.shape[axis]
        return pltpu.roll(value, by % size, axis % value.ndim)

    def source(lap_u, lap_v, u, v, feed, both):
        reaction = u * v * v
        return lap_u - reaction + feed * (1.0 - u), lap_v + reaction - both * v

    def fine_rates(buf, first, at, feed_at, count):
        laps, mids = [], []
        for field in range(2):
            f = first + field
            mid = buf[f, pl.ds(at, count), rows(), :]
            total = buf[f, pl.ds(at - 1, count), rows(), :] + buf[f, pl.ds(at + 1, count), rows(), :]
            total = total + buf[f, pl.ds(at, count), rows(-1), :] + buf[f, pl.ds(at, count), rows(1), :]
            total = total + turn(mid, 1, -1) + turn(mid, -1, -1)
            laps.append(DIFF[field] * (total - 6.0 * mid))
            mids.append(mid)
        feed = fk_buf[0, pl.ds(feed_at, count), rows(), :]
        both = fk_buf[2, pl.ds(feed_at, count), rows(), :]
        return mids, source(laps[0], laps[1], mids[0], mids[1], feed, both)

    def pair_sum(value):
        value = value + jnp.where(even_row, turn(value, -1, -2), turn(value, 1, -2))
        return value + jnp.where(even_lane, turn(value, -1, -1), turn(value, 1, -1))

    def restrict(first, second):
        return 0.125 * pair_sum(first + second)

    def coarse_rates(below, mid, above, feed, both):
        laps = []
        for field in range(2):
            total = below[field] + above[field] + turn(mid[field], 2, -2) + turn(mid[field], -2, -2)
            total = total + turn(mid[field], 2, -1) + turn(mid[field], -2, -1)
            laps.append((0.25 * DIFF[field]) * (total - 6.0 * mid[field]))
        return source(laps[0], laps[1], mid[0], mid[1], feed, both)

    def send_states(buf):
        return exchange(buf, buf.shape[0], wide, HALO, PLANES, HALO, HALO)

    arrive((s_in,))
    s_halo = send_states(first_s)
    c_halo = []
    arrive((feed_in, kill_in))
    fk_halo = exchange(fk_buf, 2, near, 4, PLANES, 4, 4)
    arrive(fk_halo)
    for p in range(0, 12, 2):
        both = fk_buf[0, pl.ds(p, 2), rows(), :] + fk_buf[1, pl.ds(p, 2), rows(), :]
        fk_buf[2, pl.ds(p, 2), rows(), :] = both
    coarse_feed, coarse_both = [], []
    for p in range(4):
        feed, kill = [restrict(fk_buf[f, 2 + 2 * p, rows(), :], fk_buf[f, 3 + 2 * p, rows(), :]) for f in range(2)]
        coarse_feed.append(feed)
        coarse_both.append(feed + kill)

    for k in range(ITERS):
        s_now, c_now = s_buf.at[k], c_buf.at[k]
        last = k == ITERS - 1
        if k > 0:
            u_old = u_buf.at[k - 1]
            arrive(u_halo)
            for p in range(0, 12, 2):
                _, one = fine_rates(u_old, 0, p + 1, p, 2)
                _, two = fine_rates(u_old, 2, p + 1, p, 2)
                for field in range(2):
                    zero = g0_buf[field, pl.ds(p, 2), rows(), :]
                    a0_buf[field, pl.ds(p, 2), rows(), :] = (
                        (WEIGHTS[0][0] - HALF_STEP) * zero + WEIGHTS[0][1] * one[field] + WEIGHTS[0][2] * two[field])
                    a1_buf[field, pl.ds(p, 2), rows(), :] = (
                        WEIGHTS[1][0] * zero + (WEIGHTS[1][1] - HALF_STEP) * one[field] + WEIGHTS[1][2] * two[field])
        arrive(s_halo)
        for p in range(0, 12, 2):
            mids, rates = fine_rates(s_now, 0, p + 1, p, 2)
            for field in range(2):
                node = mids[field] + HALF_STEP * rates[field]
                if k > 0:
                    node = node + a0_buf[field, pl.ds(p, 2), rows(), :]
                g0_buf[field, pl.ds(p, 2), rows(), :] = rates[field]
                v1_buf[field, pl.ds(p, 2), rows(), :] = node
        for p in range(0, 10, 2):
            mids, rates = fine_rates(v1_buf, 0, p + 1, p + 1, 2)
            for field in range(2):
                node = mids[field] + HALF_STEP * rates[field]
                if k > 0:
                    node = node + a1_buf[field, pl.ds(p + 1, 2), rows(), :]
                v2_buf[field, pl.ds(p, 2), rows(), :] = node
                g1_buf[field, pl.ds(p, 2), rows(), :] = rates[field]
        rest_s = [[restrict(s_now[f, 1 + 2 * p, rows(), :], s_now[f, 2 + 2 * p, rows(), :]) for f in range(2)]
                  for p in range(6)]
        if k == 0:
            coarse = rest_s
            for p in range(2, 4):
                for f in range(2):
                    c_now[f, p, rows(), :] = coarse[p][f]
        else:
            arrive(c_halo)
            coarse = [[c_now[f, p, rows(), :] for f in range(2)] for p in range(6)]
        w_one, late = [], []
        for p in range(4):
            _, two = fine_rates(v2_buf, 0, 2 * p + 1, 2 * p + 2, 2)
            rate_c = coarse_rates(coarse[p], coarse[p + 1], coarse[p + 2], coarse_feed[p], coarse_both[p])
            rate_s = coarse_rates(rest_s[p], rest_s[p + 1], rest_s[p + 2], coarse_feed[p], coarse_both[p])
            values, later_sums = [], []
            for f in range(2):
                zero = g0_buf[f, pl.ds(2 + 2 * p, 2), rows(), :]
                one = g1_buf[f, pl.ds(1 + 2 * p, 2), rows(), :]
                first, second = [w[0] * zero + w[1] * one + w[2] * two[f] for w in WEIGHTS]
                values.append(coarse[p + 1][f] + HALF_STEP * (rate_c[f] - rate_s[f]) + restrict(first[0], first[1]))
                later_sums.append(restrict(second[0], second[1]) if p in (1, 2) else None)
            w_one.append(values)
            late.append(later_sums)
        rest_v1 = [[restrict(v1_buf[f, 2 + 2 * p, rows(), :], v1_buf[f, 3 + 2 * p, rows(), :]) for f in range(2)]
                   for p in range(4)]
        keep = slice(OWN - LOW, OWN - LOW + ROWS)
        for p in (1, 2):
            rate_w = coarse_rates(w_one[p - 1], w_one[p], w_one[p + 1], coarse_feed[p], coarse_both[p])
            rate_v1 = coarse_rates(rest_v1[p - 1], rest_v1[p], rest_v1[p + 1], coarse_feed[p], coarse_both[p])
            for f in range(2):
                w_two = w_one[p][f] + HALF_STEP * (rate_w[f] - rate_v1[f]) + late[p][f]
                rest_v2 = restrict(v2_buf[f, 1 + 2 * p, rows(), :], v2_buf[f, 2 + 2 * p, rows(), :])
                for at in (2 * p - 2, 2 * p - 1):
                    two = v2_buf[f, 3 + at, rows(), :] + (w_two - rest_v2)
                    if last:
                        o_buf[f, at, :, :] = two[keep]
                    else:
                        one = v1_buf[f, 4 + at, rows(), :] + (w_one[p][f] - rest_v1[p][f])
                        u_buf[k, f, HALO + at, pl.ds(OWN, ROWS), :] = one[keep]
                        u_buf[k, 2 + f, HALO + at, pl.ds(OWN, ROWS), :] = two[keep]
                if not last:
                    w_buf[k, f, p - 1, :, :] = w_two[keep]
        if not last:
            u_now, s_next, c_next = u_buf.at[k], s_buf.at[k + 1], c_buf.at[k + 1]
            shifted = []
            for src, dst, kept in (
                (u_now.at[(pl.ds(2, 2), *own[1:])], s_next.at[own], s_now.at[own]),
                (w_buf.at[k], c_next.at[own_c], c_now.at[own_c]),
            ):
                copy, index = remote(src, dst, device(later, y))
                stay = pltpu.make_async_copy(kept, dst, recv_sem.at[index])
                onward = m < nt - 1

                @pl.when(onward)
                def _(copy=copy):
                    copy.start()

                @pl.when(m == 0)
                def _(stay=stay):
                    stay.start()

                started.append((copy, onward))
                shifted.append(copy)
            u_halo = send_states(u_now)
            arrive(shifted[:1])
            s_halo = send_states(s_next)
            arrive(shifted[1:])
            c_halo = exchange(c_next, 2, near, 2, 2, 2, 4)

    out_in = move(o_buf, out_ref.at[0], out_to, y)
    arrive((out_in,))
    for copy, when in started:
        if when is None:
            copy.wait_send()
        else:

            @pl.when(when)
            def _(copy=copy):
                copy.wait_send()

    assert used[0] <= N_SEMS


def solution(mesh):
    dims = (mesh.shape["tm"], mesh.shape["gy"], mesh.shape["gx"])

    def shards(initial_state, slice_guess, feed_rate, kill_rate):
        buffers = [
            (ITERS, 2, 14, TALL, LANES),
            (ITERS, 2, 6, TALL, LANES),
            (ITERS - 1, 4, 14, TALL, LANES),
            (ITERS - 1, 2, 2, ROWS, LANES),
            (2, 12, TALL, LANES),
            (2, 10, TALL, LANES),
            (3, 12, TALL, LANES),
            (2, 12, TALL, LANES),
            (2, 10, TALL, LANES),
            (2, 12, TALL, LANES),
            (2, 12, TALL, LANES),
            (2, PLANES, ROWS, LANES),
        ]
        return pl.pallas_call(
            functools.partial(kernel, dims),
            out_shape=jax.ShapeDtypeStruct((1, 2, PLANES, ROWS, LANES), jnp.float32),
            in_specs=[pl.BlockSpec(memory_space=pl.ANY)] * 4,
            out_specs=pl.BlockSpec(memory_space=pl.ANY),
            scratch_shapes=[pltpu.VMEM(shape, jnp.float32) for shape in buffers]
            + [pltpu.SemaphoreType.DMA((N_SEMS,)), pltpu.SemaphoreType.DMA((N_SEMS,))],
            compiler_params=pltpu.CompilerParams(collective_id=0, has_side_effects=True),
        )(initial_state, slice_guess, feed_rate, kill_rate)

    in_specs = (
        P(None, "gy", "gx", None),
        P("tm", None, "gy", "gx", None),
        P("gy", "gx", None),
        P("gy", "gx", None),
    )
    out_specs = P("tm", None, "gy", "gx", None)
    return jax.shard_map(shards, mesh=mesh, in_specs=in_specs, out_specs=out_specs, check_vma=False)
```

time: 72 us -> 67.5 us (0.938)
  the two profiles are of different devices: /device:TPU:5 before, /device:TPU:68 now
where the time goes in v2:
time: 67.5 us; the launch traced here: 67.3 us
  Pallas kernels  65.8 us (97%)
  local copies, waits for them, and re-layouts  1.47 us (2%)
    pallas_call x1, Pallas kernels, shards(): pl.pallas_call(functools.partial(kernel, dims), out_shape=jax.ShapeDtypeS...  65.8 us
    unnamed x1, local copies, waits for them, and re-layouts  1.47 us

profile of v2, /device:TPU:68, one launch (start us, length us, event | category | flops | bytes accessed | tf_op | source)
XLA Modules:
  0.0 67.3 jit_solution(16766186028837667166)
XLA Ops:
  0.0 65.8 %shard_map.46 = f32[1,2,4,16,128]{4,3,2,1,0:T(8,128)} custom-call(f32[2,4,16,128]{3,2,1,0:T(8,128)} %init_ref.1, f32[1,2,4,16,128]{4,3,2,1,0:T(8,128)} %guess_ref.1, f32[4,16,128]{2,1,0:T(8,128)} %feed_ref.1, f32[4,16,128]{2,1,0:T(8,128)} %kill_ref.1), custom_call_target="tpu_custom_call" | custom-call | tf_op jit(solution)/shard_map/pallas_call | solution.py:332
  65.8 1.5 %copy.6 = f32[1,2,4,16,128]{4,3,2,1,0:T(8,128)} copy(f32[1,2,4,16,128]{4,3,2,1,0:T(8,128)} %shard_map.46) | data formatting | bytes 131072

commit v3 on v2

--- a/solution.py
+++ b/solution.py
@@ -16,7 +16,7 @@
 TALL, LOW, WINDOW, OWN = 40, 8, 24, 12
 HALO = 5
 SHIFT = 2
-N_SEMS = 128
+N_SEMS = 144
 
 
 def kernel(dims, init_ref, guess_ref, feed_ref, kill_ref, out_ref,
@@ -56,7 +56,7 @@
     out_from = role_of(n, g)
     later, earlier = role_of((m + 1) % nt, t), role_of((m + nt - 1) % nt, t)
     near = [(dx, dy) for dx in (-1, 0, 1) for dy in (-1, 0, 1) if (dx, dy) != (0, 0)]
-    wide = near + [(dx, dy) for dx in (-2, 2) for dy in (-1, 0, 1)]
+    wide = near + [(-2, 0), (2, 0)]
 
     def neighbour(dx, dy):
         return device(role_of(m, (t + dx + ng) % ng), (y + dy + nx) % nx)
@@ -99,17 +99,19 @@
         started.append((copy, away))
         return copy
 
-    def exchange(buf, fields, where, own_x, count, width_x, width_y):
+    def exchange(buf, first, fields, where, own_x, count, width_x, width_y, corner_x, corner_y):
         copies = []
         for dx, dy in where:
+            corner = dx != 0 and dy != 0
             planes = count if dx == 0 else min(count, width_x - count * (abs(dx) - 1))
+            rows_sent = ROWS if dy == 0 else width_y
+            if corner:
+                planes, rows_sent = corner_x, corner_y
             from_x = own_x + count - planes if dx > 0 else own_x
-            to_x = from_x - dx * count
-            rows_sent = ROWS if dy == 0 else width_y
             from_y = OWN + ROWS - rows_sent if dy > 0 else OWN
-            to_y = from_y - dy * ROWS
-            src = buf.at[pl.ds(0, fields), pl.ds(from_x, planes), pl.ds(from_y, rows_sent)]
-            dst = buf.at[pl.ds(0, fields), pl.ds(to_x, planes), pl.ds(to_y, rows_sent)]
+            to_x, to_y = from_x - dx * count, from_y - dy * ROWS
+            src = buf.at[pl.ds(first, fields), pl.ds(from_x, planes), pl.ds(from_y, rows_sent)]
+            dst = buf.at[pl.ds(first, fields), pl.ds(to_x, planes), pl.ds(to_y, rows_sent)]
             copy, _ = remote(src, dst, neighbour(dx, dy))
             copy.start()
             started.append((copy, None))
@@ -177,14 +179,14 @@
             laps.append((0.25 * DIFF[field]) * (total - 6.0 * mid[field]))
         return source(laps[0], laps[1], mid[0], mid[1], feed, both)
 
-    def send_states(buf):
-        return exchange(buf, buf.shape[0], wide, HALO, PLANES, HALO, HALO)
+    def send_states(buf, first, fields):
+        return exchange(buf, first, fields, wide, HALO, PLANES, HALO, HALO, 4, 4)
 
     arrive((s_in,))
-    s_halo = send_states(first_s)
+    s_halo = send_states(first_s, 0, 2)
     c_halo = []
     arrive((feed_in, kill_in))
-    fk_halo = exchange(fk_buf, 2, near, 4, PLANES, 4, 4)
+    fk_halo = exchange(fk_buf, 0, 2, near, 4, PLANES, 4, 4, 3, 3)
     arrive(fk_halo)
     for p in range(0, 12, 2):
         both = fk_buf[0, pl.ds(p, 2), rows(), :] + fk_buf[1, pl.ds(p, 2), rows(), :]
@@ -274,7 +276,8 @@
             u_now, s_next, c_next = u_buf.at[k], s_buf.at[k + 1], c_buf.at[k + 1]
             shifted = []
             for src, dst, kept in (
-                (u_now.at[(pl.ds(2, 2), *own[1:])], s_next.at[own], s_now.at[own]),
+                (u_now.at[(pl.ds(2, 1), *own[1:])], s_next.at[(pl.ds(0, 1), *own[1:])], s_now.at[(pl.ds(0, 1), *own[1:])]),
+                (u_now.at[(pl.ds(3, 1), *own[1:])], s_next.at[(pl.ds(1, 1), *own[1:])], s_now.at[(pl.ds(1, 1), *own[1:])]),
                 (w_buf.at[k], c_next.at[own_c], c_now.at[own_c]),
             ):
                 copy, index = remote(src, dst, device(later, y))
@@ -291,11 +294,13 @@
 
                 started.append((copy, onward))
                 shifted.append(copy)
-            u_halo = send_states(u_now)
-            arrive(shifted[:1])
-            s_halo = send_states(s_next)
-            arrive(shifted[1:])
-            c_halo = exchange(c_next, 2, near, 2, 2, 2, 4)
+            u_halo = send_states(u_now, 0, 4)
+            s_halo = []
+            for field in range(2):
+                arrive(shifted[field : field + 1])
+                s_halo += send_states(s_next, field, 1)
+            arrive(shifted[2:])
+            c_halo = exchange(c_next, 0, 2, near, 2, 2, 2, 4, 1, 2)
 
     out_in = move(o_buf, out_ref.at[0], out_to, y)
     arrive((out_in,))

time: 67.5 us -> 65.4 us (0.969)
  Pallas kernels: 65.8 us -> 63.7 us
    pallas_call x1, Pallas kernels: 65.8 us -> 63.7 us  [shards(): pl.pallas_call(functools.partial(kernel, dims), out_shape=jax.ShapeDtypeS...]
where the time goes in v3:
time: 65.4 us; the launch traced here: 65.2 us
  Pallas kernels  63.7 us (97%)
  local copies, waits for them, and re-layouts  1.47 us (2%)
    pallas_call x1, Pallas kernels, shards(): pl.pallas_call(functools.partial(kernel, dims), out_shape=jax.ShapeDtypeS...  63.7 us
    unnamed x1, local copies, waits for them, and re-layouts  1.47 us

profile of v3, /device:TPU:68, one launch (start us, length us, event | category | flops | bytes accessed | tf_op | source)
XLA Modules:
  0.0 65.2 jit_solution(2751045324896918262)
XLA Ops:
  0.0 63.7 %shard_map.46 = f32[1,2,4,16,128]{4,3,2,1,0:T(8,128)} custom-call(f32[2,4,16,128]{3,2,1,0:T(8,128)} %init_ref.1, f32[1,2,4,16,128]{4,3,2,1,0:T(8,128)} %guess_ref.1, f32[4,16,128]{2,1,0:T(8,128)} %feed_ref.1, f32[4,16,128]{2,1,0:T(8,128)} %kill_ref.1), custom_call_target="tpu_custom_call" | custom-call | tf_op jit(solution)/shard_map/pallas_call | solution.py:337
  63.7 1.5 %copy.6 = f32[1,2,4,16,128]{4,3,2,1,0:T(8,128)} copy(f32[1,2,4,16,128]{4,3,2,1,0:T(8,128)} %shard_map.46) | data formatting | bytes 131072

commit v4 on v3

--- a/solution.py
+++ b/solution.py
@@ -16,12 +16,12 @@
 TALL, LOW, WINDOW, OWN = 40, 8, 24, 12
 HALO = 5
 SHIFT = 2
-N_SEMS = 144
+N_SEMS = 160
 
 
 def kernel(dims, init_ref, guess_ref, feed_ref, kill_ref, out_ref,
            s_buf, c_buf, u_buf, w_buf, v1_buf, v2_buf, fk_buf, g0_buf, g1_buf, a0_buf, a1_buf, o_buf,
-           send_sem, recv_sem):
+           send_sem, recv_sem, home_sem):
     nt, ng, nx = dims
     chips = ng // 2
     blocks = nt // ng
@@ -53,16 +53,15 @@
     fk_at = (along - t + ng // 2 + nt) % nt
     fk_from = (2 * blocks * ((t // 2 + (fk_at % ng) // 2) % chips) + 2 * (fk_at // ng) + fk_at % 2, t)
     out_to = home_of(m, t)
-    out_from = role_of(n, g)
     later, earlier = role_of((m + 1) % nt, t), role_of((m + nt - 1) % nt, t)
-    near = [(dx, dy) for dx in (-1, 0, 1) for dy in (-1, 0, 1) if (dx, dy) != (0, 0)]
-    wide = near + [(-2, 0), (2, 0)]
+    near = [(-1, -1), (-1, 1), (1, -1), (1, 1), (-1, 0), (1, 0), (0, -1), (0, 1)]
+    wide = near[:6] + [(-2, 0), (2, 0)] + near[6:]
 
     def neighbour(dx, dy):
         return device(role_of(m, (t + dx + ng) % ng), (y + dy + nx) % nx)
 
     barrier = pltpu.get_barrier_semaphore()
-    partners = [device(place, y) for place in (s_from, fk_from, out_from, earlier, later)]
+    partners = [device(place, y) for place in (s_from, fk_from, earlier, later)]
     partners += [neighbour(dx, dy) for dx, dy in wide]
     for partner in partners:
         pl.semaphore_signal(barrier, inc=1, device_id=partner, device_id_type=pl.DeviceIdType.MESH)
@@ -128,10 +127,13 @@
     fk_own = (pl.ds(4, PLANES), pl.ds(OWN, ROWS))
     first_s = s_buf.at[0]
     last_home = n == nt - 1
-    mark = used[0]
-    s_in = move(guess_ref.at[0], first_s.at[own], s_to, y, jnp.logical_not(last_home))
-    used[0] = mark
-    move(init_ref, first_s.at[own], s_to, y, last_home)
+    s_in = []
+    for field in range(2):
+        part = (field, *own[1:])
+        mark = used[0]
+        s_in.append(move(guess_ref.at[0, field], first_s.at[part], s_to, y, jnp.logical_not(last_home)))
+        used[0] = mark
+        move(init_ref.at[field], first_s.at[part], s_to, y, last_home)
     feed_in = move(feed_ref, fk_buf.at[(0, *fk_own)], fk_to, y)
     kill_in = move(kill_ref, fk_buf.at[(1, *fk_own)], fk_to, y)
 
@@ -182,11 +184,14 @@
     def send_states(buf, first, fields):
         return exchange(buf, first, fields, wide, HALO, PLANES, HALO, HALO, 4, 4)
 
-    arrive((s_in,))
-    s_halo = send_states(first_s, 0, 2)
-    c_halo = []
-    arrive((feed_in, kill_in))
-    fk_halo = exchange(fk_buf, 0, 2, near, 4, PLANES, 4, 4, 3, 3)
+    s_halo, c_halo, fk_halo = [], [], []
+    for field in range(2):
+        arrive((s_in[field],))
+        s_halo += send_states(first_s, field, 1)
+    pl.semaphore_signal(home_sem, inc=1, device_id=device(earlier, y), device_id_type=pl.DeviceIdType.MESH)
+    for field, moved in enumerate((feed_in, kill_in)):
+        arrive((moved,))
+        fk_halo += exchange(fk_buf, field, 1, near, 4, PLANES, 4, 4, 3, 3)
     arrive(fk_halo)
     for p in range(0, 12, 2):
         both = fk_buf[0, pl.ds(p, 2), rows(), :] + fk_buf[1, pl.ds(p, 2), rows(), :]
@@ -302,6 +307,7 @@
             arrive(shifted[2:])
             c_halo = exchange(c_next, 0, 2, near, 2, 2, 2, 4, 1, 2)
 
+    pl.semaphore_wait(home_sem, 1)
     out_in = move(o_buf, out_ref.at[0], out_to, y)
     arrive((out_in,))
     for copy, when in started:
@@ -340,7 +346,7 @@
             in_specs=[pl.BlockSpec(memory_space=pl.ANY)] * 4,
             out_specs=pl.BlockSpec(memory_space=pl.ANY),
             scratch_shapes=[pltpu.VMEM(shape, jnp.float32) for shape in buffers]
-            + [pltpu.SemaphoreType.DMA((N_SEMS,)), pltpu.SemaphoreType.DMA((N_SEMS,))],
+            + [pltpu.SemaphoreType.DMA((N_SEMS,)), pltpu.SemaphoreType.DMA((N_SEMS,)), pltpu.SemaphoreType.REGULAR],
             compiler_params=pltpu.CompilerParams(collective_id=0, has_side_effects=True),
         )(initial_state, slice_guess, feed_rate, kill_rate)
 

time: 65.4 us -> 63.7 us (0.974)
  Pallas kernels: 63.7 us -> 62.1 us
    pallas_call x1, Pallas kernels: 63.7 us -> 62.1 us  [shards(): pl.pallas_call(functools.partial(kernel, dims), out_shape=jax.ShapeDtypeS...]
where the time goes in v4:
time: 63.7 us; the launch traced here: 63.5 us
  Pallas kernels  62.1 us (97%)
  local copies, waits for them, and re-layouts  1.47 us (2%)
    pallas_call x1, Pallas kernels, shards(): pl.pallas_call(functools.partial(kernel, dims), out_shape=jax.ShapeDtypeS...  62.1 us
    unnamed x1, local copies, waits for them, and re-layouts  1.47 us

profile of v4, /device:TPU:68, one launch (start us, length us, event | category | flops | bytes accessed | tf_op | source)
XLA Modules:
  0.0 63.5 jit_solution(3191860424260420996)
XLA Ops:
  0.0 62.1 %shard_map.46 = f32[1,2,4,16,128]{4,3,2,1,0:T(8,128)} custom-call(f32[2,4,16,128]{3,2,1,0:T(8,128)} %init_ref.1, f32[1,2,4,16,128]{4,3,2,1,0:T(8,128)} %guess_ref.1, f32[4,16,128]{2,1,0:T(8,128)} %feed_ref.1, f32[4,16,128]{2,1,0:T(8,128)} %kill_ref.1), custom_call_target="tpu_custom_call" | custom-call | tf_op jit(solution)/shard_map/pallas_call | solution.py:343
  62.1 1.5 %copy.6 = f32[1,2,4,16,128]{4,3,2,1,0:T(8,128)} copy(f32[1,2,4,16,128]{4,3,2,1,0:T(8,128)} %shard_map.46) | data formatting | bytes 131072

commit v5 on v4

--- a/solution.py
+++ b/solution.py
@@ -15,7 +15,7 @@
 PLANES, ROWS, LANES = 4, 16, 128
 TALL, LOW, WINDOW, OWN = 40, 8, 24, 12
 HALO = 5
-SHIFT = 2
+SHIFT = 8
 N_SEMS = 160
 
 
@@ -32,7 +32,7 @@
 
     def role_of(slice_at, tile):
         along = (slice_at + SHIFT) % nt
-        turned = (tile + 2 * (slice_at // (2 * blocks))) % ng
+        turned = tile
         return 2 * blocks * (turned // 2) + 2 * (along // ng) + turned % 2, along % ng
 
     def device(place, column):
@@ -44,7 +44,7 @@
     across, block, core = n // (2 * blocks), (n // 2) % blocks, n % 2
     along = ng * block + g
     m = (along + nt - SHIFT) % nt
-    t = (2 * across + core + ng - 2 * (m // (2 * blocks))) % ng
+    t = (2 * across + core + ng) % ng
 
     s_to = role_of((n + 1) % nt, g)
     s_from = home_of((m + nt - 1) % nt, t)
@@ -57,12 +57,12 @@
     near = [(-1, -1), (-1, 1), (1, -1), (1, 1), (-1, 0), (1, 0), (0, -1), (0, 1)]
     wide = near[:6] + [(-2, 0), (2, 0)] + near[6:]
 
-    def neighbour(dx, dy):
-        return device(role_of(m, (t + dx + ng) % ng), (y + dy + nx) % nx)
+    def neighbour(dx, dy, ahead=0):
+        return device(role_of((m + ahead + nt) % nt, (t + dx + ng) % ng), (y + dy + nx) % nx)
 
     barrier = pltpu.get_barrier_semaphore()
-    partners = [device(place, y) for place in (s_from, fk_from, earlier, later)]
-    partners += [neighbour(dx, dy) for dx, dy in wide]
+    partners = [device(place, y) for place in (s_from, fk_from, later)]
+    partners += [neighbour(dx, dy) for dx, dy in wide] + [neighbour(dx, dy, -1) for dx, dy in [(0, 0)] + near]
     for partner in partners:
         pl.semaphore_signal(barrier, inc=1, device_id=partner, device_id_type=pl.DeviceIdType.MESH)
     pl.semaphore_wait(barrier, len(partners))
@@ -98,31 +98,49 @@
         started.append((copy, away))
         return copy
 
-    def exchange(buf, first, fields, where, own_x, count, width_x, width_y, corner_x, corner_y):
+    def piece(dx, dy, own_x, count, width_x, width_y, corner_x, corner_y):
+        planes = count if dx == 0 else min(count, width_x - count * (abs(dx) - 1))
+        rows_sent = ROWS if dy == 0 else width_y
+        if dx != 0 and dy != 0:
+            planes, rows_sent = corner_x, corner_y
+        from_x = own_x + count - planes if dx > 0 else own_x
+        from_y = OWN + ROWS - rows_sent if dy > 0 else OWN
+        to_x, to_y = from_x - dx * count, from_y - dy * ROWS
+        return (pl.ds(from_x, planes), pl.ds(from_y, rows_sent)), (pl.ds(to_x, planes), pl.ds(to_y, rows_sent))
+
+    def exchange(buf, first, fields, where, *sizes):
         copies = []
         for dx, dy in where:
-            corner = dx != 0 and dy != 0
-            planes = count if dx == 0 else min(count, width_x - count * (abs(dx) - 1))
-            rows_sent = ROWS if dy == 0 else width_y
-            if corner:
-                planes, rows_sent = corner_x, corner_y
-            from_x = own_x + count - planes if dx > 0 else own_x
-            from_y = OWN + ROWS - rows_sent if dy > 0 else OWN
-            to_x, to_y = from_x - dx * count, from_y - dy * ROWS
-            src = buf.at[pl.ds(first, fields), pl.ds(from_x, planes), pl.ds(from_y, rows_sent)]
-            dst = buf.at[pl.ds(first, fields), pl.ds(to_x, planes), pl.ds(to_y, rows_sent)]
-            copy, _ = remote(src, dst, neighbour(dx, dy))
+            src, dst = piece(dx, dy, *sizes)
+            copy, _ = remote(buf.at[(pl.ds(first, fields), *src)], buf.at[(pl.ds(first, fields), *dst)], neighbour(dx, dy))
             copy.start()
             started.append((copy, None))
             copies.append(copy)
         return copies
 
+    onward = m < nt - 1
+
+    def hand_on(src, dst, kept, dx=0, dy=0):
+        copy, index = remote(src, dst, neighbour(dx, dy, 1))
+        stay = pltpu.make_async_copy(kept, dst, recv_sem.at[index])
+
+        @pl.when(onward)
+        def _():
+            copy.start()
+
+        @pl.when(m == 0)
+        def _():
+            stay.start()
+
+        started.append((copy, onward))
+        return copy
+
     def arrive(copies):
         for copy in copies:
             copy.wait_recv()
 
     own = (pl.ds(0, 2), pl.ds(HALO, PLANES), pl.ds(OWN, ROWS))
-    own_c = (pl.ds(0, 2), pl.ds(2, 2), pl.ds(OWN, ROWS))
+    s_sizes = (HALO, PLANES, HALO, HALO, 4, 4)
 
     fk_own = (pl.ds(4, PLANES), pl.ds(OWN, ROWS))
     first_s = s_buf.at[0]
@@ -181,8 +199,17 @@
             laps.append((0.25 * DIFF[field]) * (total - 6.0 * mid[field]))
         return source(laps[0], laps[1], mid[0], mid[1], feed, both)
 
+    def pack(planes):
+        mixed = [jnp.where(even_lane, plane[0], plane[1]) for plane in planes]
+        return jnp.where(even_row, mixed[0], mixed[1])
+
+    def unpack(packed):
+        planes = [jnp.where(even_row, packed, turn(packed, 1, -2)), jnp.where(even_row, turn(packed, -1, -2), packed)]
+        return [[jnp.where(even_lane, plane, turn(plane, 1, -1)), jnp.where(even_lane, turn(plane, -1, -1), plane)]
+                for plane in planes]
+
     def send_states(buf, first, fields):
-        return exchange(buf, first, fields, wide, HALO, PLANES, HALO, HALO, 4, 4)
+        return exchange(buf, first, fields, wide, *s_sizes)
 
     s_halo, c_halo, fk_halo = [], [], []
     for field in range(2):
@@ -238,12 +265,11 @@
                   for p in range(6)]
         if k == 0:
             coarse = rest_s
-            for p in range(2, 4):
-                for f in range(2):
-                    c_now[f, p, rows(), :] = coarse[p][f]
+            for p in range(3):
+                c_now[p, rows(), :] = pack(coarse[2 * p : 2 * p + 2])
         else:
             arrive(c_halo)
-            coarse = [[c_now[f, p, rows(), :] for f in range(2)] for p in range(6)]
+            coarse = [plane for p in range(3) for plane in unpack(c_now[p, rows(), :])]
         w_one, late = [], []
         for p in range(4):
             _, two = fine_rates(v2_buf, 0, 2 * p + 1, 2 * p + 2, 2)
@@ -261,51 +287,45 @@
         rest_v1 = [[restrict(v1_buf[f, 2 + 2 * p, rows(), :], v1_buf[f, 3 + 2 * p, rows(), :]) for f in range(2)]
                    for p in range(4)]
         keep = slice(OWN - LOW, OWN - LOW + ROWS)
+        w_two = []
         for p in (1, 2):
+            w_two.append([])
             rate_w = coarse_rates(w_one[p - 1], w_one[p], w_one[p + 1], coarse_feed[p], coarse_both[p])
             rate_v1 = coarse_rates(rest_v1[p - 1], rest_v1[p], rest_v1[p + 1], coarse_feed[p], coarse_both[p])
             for f in range(2):
-                w_two = w_one[p][f] + HALF_STEP * (rate_w[f] - rate_v1[f]) + late[p][f]
+                w_end = w_one[p][f] + HALF_STEP * (rate_w[f] - rate_v1[f]) + late[p][f]
+                w_two[-1].append(w_end)
                 rest_v2 = restrict(v2_buf[f, 1 + 2 * p, rows(), :], v2_buf[f, 2 + 2 * p, rows(), :])
                 for at in (2 * p - 2, 2 * p - 1):
-                    two = v2_buf[f, 3 + at, rows(), :] + (w_two - rest_v2)
+                    two = v2_buf[f, 3 + at, rows(), :] + (w_end - rest_v2)
                     if last:
                         o_buf[f, at, :, :] = two[keep]
                     else:
                         one = v1_buf[f, 4 + at, rows(), :] + (w_one[p][f] - rest_v1[p][f])
                         u_buf[k, f, HALO + at, pl.ds(OWN, ROWS), :] = one[keep]
                         u_buf[k, 2 + f, HALO + at, pl.ds(OWN, ROWS), :] = two[keep]
-                if not last:
-                    w_buf[k, f, p - 1, :, :] = w_two[keep]
         if not last:
+            w_buf[k, :, :] = pack(w_two)[keep]
             u_now, s_next, c_next = u_buf.at[k], s_buf.at[k + 1], c_buf.at[k + 1]
-            shifted = []
-            for src, dst, kept in (
-                (u_now.at[(pl.ds(2, 1), *own[1:])], s_next.at[(pl.ds(0, 1), *own[1:])], s_now.at[(pl.ds(0, 1), *own[1:])]),
-                (u_now.at[(pl.ds(3, 1), *own[1:])], s_next.at[(pl.ds(1, 1), *own[1:])], s_now.at[(pl.ds(1, 1), *own[1:])]),
-                (w_buf.at[k], c_next.at[own_c], c_now.at[own_c]),
-            ):
-                copy, index = remote(src, dst, device(later, y))
-                stay = pltpu.make_async_copy(kept, dst, recv_sem.at[index])
-                onward = m < nt - 1
-
-                @pl.when(onward)
-                def _(copy=copy):
-                    copy.start()
-
-                @pl.when(m == 0)
-                def _(stay=stay):
-                    stay.start()
-
-                started.append((copy, onward))
-                shifted.append(copy)
+            shifted = [
+                hand_on(u_now.at[(2 + f, *own[1:])], s_next.at[(f, *own[1:])], s_now.at[(f, *own[1:])]) for f in range(2)
+            ]
+            s_halo = []
+            for dx, dy in near:
+                if dx != 0 and dy != 0:
+                    src, dst = piece(dx, dy, *s_sizes)
+                    src, dst = (pl.ds(2, 2), *src), (pl.ds(0, 2), *dst)
+                    s_halo.append(hand_on(u_now.at[src], s_next.at[dst], s_now.at[dst], dx, dy))
+            c_halo = []
+            for dx, dy in [(0, 0)] + near:
+                sent = ROWS if dy == 0 else 4
+                from_y = ROWS - sent if dy > 0 else 0
+                src, dst = pl.ds(from_y, sent), (1 - dx, pl.ds(OWN + from_y - dy * ROWS, sent))
+                c_halo.append(hand_on(w_buf.at[k, src], c_next.at[dst], c_now.at[dst], dx, dy))
             u_halo = send_states(u_now, 0, 4)
-            s_halo = []
             for field in range(2):
                 arrive(shifted[field : field + 1])
-                s_halo += send_states(s_next, field, 1)
-            arrive(shifted[2:])
-            c_halo = exchange(c_next, 0, 2, near, 2, 2, 2, 4, 1, 2)
+                s_halo += exchange(s_next, field, 1, wide[4:], *s_sizes)
 
     pl.semaphore_wait(home_sem, 1)
     out_in = move(o_buf, out_ref.at[0], out_to, y)
@@ -328,9 +348,9 @@
     def shards(initial_state, slice_guess, feed_rate, kill_rate):
         buffers = [
             (ITERS, 2, 14, TALL, LANES),
-            (ITERS, 2, 6, TALL, LANES),
+            (ITERS, 3, TALL, LANES),
             (ITERS - 1, 4, 14, TALL, LANES),
-            (ITERS - 1, 2, 2, ROWS, LANES),
+            (ITERS - 1, ROWS, LANES),
             (2, 12, TALL, LANES),
             (2, 10, TALL, LANES),
             (3, 12, TALL, LANES),

time: 63.7 us -> 62.6 us (0.983)
  the two profiles are of different devices: /device:TPU:68 before, /device:TPU:1 now
where the time goes in v5:
time: 62.6 us; the launch traced here: 62.4 us
  Pallas kernels  60.9 us (97%)
  local copies, waits for them, and re-layouts  1.47 us (2%)
    pallas_call x1, Pallas kernels, shards(): pl.pallas_call(functools.partial(kernel, dims), out_shape=jax.ShapeDtypeS...  60.9 us
    unnamed x1, local copies, waits for them, and re-layouts  1.47 us

profile of v5, /device:TPU:1, one launch (start us, length us, event | category | flops | bytes accessed | tf_op | source)
XLA Modules:
  0.0 62.4 jit_solution(16401839508807441823)
XLA Ops:
  0.0 60.9 %shard_map.46 = f32[1,2,4,16,128]{4,3,2,1,0:T(8,128)} custom-call(f32[2,4,16,128]{3,2,1,0:T(8,128)} %init_ref.1, f32[1,2,4,16,128]{4,3,2,1,0:T(8,128)} %guess_ref.1, f32[4,16,128]{2,1,0:T(8,128)} %feed_ref.1, f32[4,16,128]{2,1,0:T(8,128)} %kill_ref.1), custom_call_target="tpu_custom_call" | custom-call | tf_op jit(solution)/shard_map/pallas_call | solution.py:363
  60.9 1.5 %copy.6 = f32[1,2,4,16,128]{4,3,2,1,0:T(8,128)} copy(f32[1,2,4,16,128]{4,3,2,1,0:T(8,128)} %shard_map.46) | data formatting | bytes 131072

commit v6 on v5

--- a/solution.py
+++ b/solution.py
@@ -15,7 +15,7 @@
 PLANES, ROWS, LANES = 4, 16, 128
 TALL, LOW, WINDOW, OWN = 40, 8, 24, 12
 HALO = 5
-SHIFT = 8
+SHIFT = 9
 N_SEMS = 160
 
 

time: 62.6 us -> 62.3 us (level)
  the two profiles are of different devices: /device:TPU:1 before, /device:TPU:3 now
where the time goes in v6:
time: 62.3 us; the launch traced here: 62.1 us
  Pallas kernels  60.6 us (97%)
  local copies, waits for them, and re-layouts  1.47 us (2%)
    pallas_call x1, Pallas kernels, shards(): pl.pallas_call(functools.partial(kernel, dims), out_shape=jax.ShapeDtypeS...  60.6 us
    unnamed x1, local copies, waits for them, and re-layouts  1.47 us

profile of v6, /device:TPU:3, one launch (start us, length us, event | category | flops | bytes accessed | tf_op | source)
XLA Modules:
  0.0 62.1 jit_solution(2950112792750962260)
XLA Ops:
  0.0 60.6 %shard_map.46 = f32[1,2,4,16,128]{4,3,2,1,0:T(8,128)} custom-call(f32[2,4,16,128]{3,2,1,0:T(8,128)} %init_ref.1, f32[1,2,4,16,128]{4,3,2,1,0:T(8,128)} %guess_ref.1, f32[4,16,128]{2,1,0:T(8,128)} %feed_ref.1, f32[4,16,128]{2,1,0:T(8,128)} %kill_ref.1), custom_call_target="tpu_custom_call" | custom-call | tf_op jit(solution)/shard_map/pallas_call | solution.py:363
  60.6 1.5 %copy.6 = f32[1,2,4,16,128]{4,3,2,1,0:T(8,128)} copy(f32[1,2,4,16,128]{4,3,2,1,0:T(8,128)} %shard_map.46) | data formatting | bytes 131072
